TPU v7x, 512 devices: a whole 4x4x16 slice. The times are simulated.
512 devices in a mesh: replica: 32 (over z_lo, y, core), tensor: 16 (over z_hi, x).
Axes of the slice: x: 4, y: 4, z: 16 (z_hi: 4, z_lo: 4; z = z_hi * 4 + z_lo), core: 2. Of those that a mesh axis runs over, the one named last changes fastest.
Arguments:
- queries: bfloat16 [1024, 4, 8192], P('replica', None, 'tensor'), may hold values from -64 to 64
- new_keys: bfloat16 [1024, 4, 2048], P('replica', None, 'tensor'), may hold values from -6 to 6, as said below
- new_values: bfloat16 [1024, 4, 2048], P('replica', None, 'tensor'), may hold values from -6 to 6, as said below
- cache_keys: bfloat16 [1024, 128, 2048], P('replica', None, 'tensor'), may hold values from -6 to 6, as said below
- cache_values: bfloat16 [1024, 128, 2048], P('replica', None, 'tensor'), may hold values from -6 to 6, as said below
- serve_lists: int32 [32, 32], replicated, may hold values from 0 to 1023, as said below
- turn_lens: int32 [1024], replicated, may hold values from 1 to 4, 2560 in all
- cache_lens: int32 [1024], P('replica'), may hold values from 1 to 128, 65536 in all
- owner_map: int32 [32], replicated, may hold values from 0 to 31, each once
- new_wo: bfloat16 [32, 256, 5120], P('replica', 'tensor'), may hold values from -0.0625 to 0.0625
Outputs:
- projected: bfloat16 [32, 128, 5120], P('replica', 'tensor')
Inputs may be any that keep to these rules, and one draw needn't show every extreme that they name: `serve_lists`: row r lists the trajectories whose caches replica r holds, one a slot; every trajectory id appears once, and each row holds exactly one id of every block of 32 consecutive ids. `new_keys`: column block j equals column block (j // 2) * 2: 8 distinct heads, each stored 2 times. `new_values`: column block j equals column block (j // 2) * 2: 8 distinct heads, each stored 2 times. `cache_keys`: column block j equals column block (j // 2) * 2: 8 distinct heads, each stored 2 times. `cache_values`: column block j equals column block (j // 2) * 2: 8 distinct heads, each stored 2 times.
All inputs are finite; a program needn't handle non-finite values. No bound on the sum of `cache_lens` on one device may be relied on, other than what follows from the above.
Results may differ from a plain program's by a relative error of at most 0.019.
Values may be sent and summed in bfloat16 or wider, within the bound.
No kernel may reach another device: no remote copies, remote signals or barrier semaphores. Data moves between devices by JAX's collectives and lax.ppermute only.
A program may use at most 64 MiB of HBM per device.

v0:
```python
import math

import jax
import jax.numpy as jnp
from jax import lax
from jax.sharding import PartitionSpec as P

HD = 128


def attend(query_rows, key_rows, value_rows, cache_k, cache_v, live_turn, live_cache):
    slot_count, turn_size, query_cols = query_rows.shape
    cache_size = cache_k.shape[1]
    key_blocks = key_rows.shape[2] // HD
    group_size = query_cols // HD // key_blocks
    all_keys = jnp.concatenate([cache_k, key_rows], axis=1).reshape(
        slot_count, cache_size + turn_size, key_blocks, HD
    )
    all_values = jnp.concatenate([cache_v, value_rows], axis=1).reshape(
        slot_count, cache_size + turn_size, key_blocks, HD
    )
    grouped = query_rows.reshape(slot_count, turn_size, key_blocks, group_size, HD)
    scores = jnp.einsum(
        "bpkgd,bckd->bkgpc", grouped, all_keys, preferred_element_type=jnp.float32
    ) / math.sqrt(HD)
    positions = jnp.arange(cache_size + turn_size, dtype=jnp.int32)
    query_pos = jnp.arange(turn_size, dtype=jnp.int32)
    allowed = jnp.where(
        positions[None, None, :] < cache_size,
        positions[None, None, :] < live_cache[:, None, None],
        positions[None, None, :] - cache_size <= query_pos[None, :, None],
    )
    scores = jnp.where(allowed[:, None, None, :, :], scores, -jnp.inf)
    row_max = jnp.max(scores, axis=-1, keepdims=True)
    exponent = jnp.exp(scores - row_max)
    soft_weights = (exponent / jnp.sum(exponent, axis=-1, keepdims=True)).astype(jnp.bfloat16)
    mixed_values = jnp.einsum(
        "bkgpc,bckd->bpkgd", soft_weights, all_values, preferred_element_type=jnp.float32
    )
    live_rows = query_pos[None, :] < live_turn[:, None]
    mixed_values = jnp.where(live_rows[:, :, None, None, None], mixed_values, 0.0)
    return mixed_values.astype(jnp.bfloat16).reshape(slot_count, turn_size, query_cols)


def on_device(
    queries,
    new_keys,
    new_values,
    cache_keys,
    cache_values,
    serve_lists,
    turn_lens,
    cache_lens,
    owner_map,
    new_wo,
):
    replicas = lax.axis_size("replica")
    own_replica = lax.axis_index("replica")
    sources = serve_lists // replicas
    chosen = serve_lists % replicas
    send_index = jnp.sum(jnp.where(sources == own_replica, chosen, 0), axis=1)
    outgoing = (
        jnp.take(queries, send_index, axis=0),
        jnp.take(new_keys, send_index, axis=0),
        jnp.take(new_values, send_index, axis=0),
    )
    arrived = (
        lax.all_to_all(outgoing[0], "replica", split_axis=0, concat_axis=0, tiled=True),
        lax.all_to_all(outgoing[1], "replica", split_axis=0, concat_axis=0, tiled=True),
        lax.all_to_all(outgoing[2], "replica", split_axis=0, concat_axis=0, tiled=True),
    )
    served = jnp.take(serve_lists, own_replica, axis=0)
    anchor = served // replicas
    slot_q = jnp.take(arrived[0], anchor, axis=0)
    slot_k = jnp.take(arrived[1], anchor, axis=0)
    slot_v = jnp.take(arrived[2], anchor, axis=0)
    turn_live = jnp.take(turn_lens, served)
    attended = attend(slot_q, slot_k, slot_v, cache_keys, cache_values, turn_live, cache_lens)
    flat_rows = attended.reshape(-1, attended.shape[2])
    out_width = new_wo.shape[2]
    total_rows = flat_rows.shape[0]
    share_rows = total_rows // lax.axis_size("tensor")
    gathered = lax.all_gather(new_wo, "replica", axis=0, tiled=True)
    w_slice = jnp.take(gathered, owner_map, axis=0).reshape(-1, out_width)
    projected = lax.psum_scatter(
        jnp.dot(flat_rows, w_slice, preferred_element_type=jnp.float32).astype(jnp.bfloat16),
        "tensor",
        scatter_dimension=0,
        tiled=True,
    )
    return projected.reshape(1, share_rows, out_width)


def solution(mesh):
    placed = (
        P("replica", None, "tensor"),
        P("replica", None, "tensor"),
        P("replica", None, "tensor"),
        P("replica", None, "tensor"),
        P("replica", None, "tensor"),
        P(),
        P(),
        P("replica"),
        P(),
        P("replica", "tensor", None),
    )
    return jax.shard_map(
        on_device,
        mesh=mesh,
        in_specs=placed,
        out_specs=P("replica", "tensor", None),
        check_vma=False,
    )
```

profile of v0, /device:TPU:16, one launch (start us, length us, event | category | flops | bytes accessed | tf_op | source)
XLA Modules:
  0.0 218.5 jit_solution(12812036573018416252)
XLA Ops:
  6.5 0.7 all-gather.2.cloned.1.call-update
  7.3 0.8 fusion.16
  8.1 1.4 gather_fusion.4
  9.5 1.4 gather_fusion.2
  10.9 0.7 broadcast_select_fusion.6
  11.6 9.2 %all-to-all-start.1 = ((bf16[32,4,128]{2,1,0:T(4,128)(2,1)}), bf16[32,4,128]{2,1,0:T(4,128)(2,1)S(1)}, u32[]{:S(2)}, u32[]{:S(2)}) async-start(bf16[32,4,128]{2,1,0:T(4,128)(2,1)} %get-tuple-element.24), calls=%async_computation.1 | async-start | bytes 65536 | tf_op jit(solution)/shard_map/all_to_all | solution.py:69
  20.9 0.7 gather_fusion.6
  21.6 0.7 fusion.19
  22.3 1.4 gather_fusion
  23.7 0.7 compare_select_fusion.2
  24.4 0.7 iota_compare_fusion
  25.2 0.8 broadcast_select_fusion.2
  26.0 0.7 compare_and_fusion.2
  26.6 7.8 %all-to-all-start = ((bf16[32,4,128]{2,1,0:T(4,128)(2,1)}), bf16[32,4,128]{2,1,0:T(4,128)(2,1)S(1)}, u32[]{:S(2)}, u32[]{:S(2)}) async-start(bf16[32,4,128]{2,1,0:T(4,128)(2,1)} %get-tuple-element.25), calls=%async_computation | async-start | bytes 65536 | tf_op jit(solution)/shard_map/all_to_all | solution.py:70
  34.5 5.6 %all-to-all-done = bf16[32,4,128]{2,1,0:T(4,128)(2,1)S(1)} async-done(((bf16[32,4,128]{2,1,0:T(4,128)(2,1)}), bf16[32,4,128]{2,1,0:T(4,128)(2,1)S(1)}, u32[]{:S(2)}, u32[]{:S(2)}) %all-to-all-start) | async-done | bytes 32800 | tf_op jit(solution)/shard_map/all_to_all | solution.py:70
  40.1 5.9 %all-to-all-start.2 = ((bf16[32,4,512]{2,1,0:T(4,128)(2,1)}), bf16[32,4,512]{2,1,0:T(4,128)(2,1)S(1)}, u32[]{:S(2)}, u32[]{:S(2)}) async-start(bf16[32,4,512]{2,1,0:T(4,128)(2,1)} %broadcast_select_fusion.2), calls=%async_computation.2 | async-start | bytes 262144 | tf_op jit(solution)/shard_map/all_to_all | solution.py:68
  47.5 5.8 %all-to-all-done.2 = bf16[32,4,512]{2,1,0:T(4,128)(2,1)S(1)} async-done(((bf16[32,4,512]{2,1,0:T(4,128)(2,1)}), bf16[32,4,512]{2,1,0:T(4,128)(2,1)S(1)}, u32[]{:S(2)}, u32[]{:S(2)}) %all-to-all-start.2) | async-done | bytes 131104 | tf_op jit(solution)/shard_map/all_to_all | solution.py:68
  53.3 0.7 gather_fusion.7
  54.2 0.9 fusion.22
  56.4 28.9 %all-gather.2.cloned.1.call-done = bf16[32,16,5120]{2,1,0:T(8,128)(2,1)} async-done(((bf16[1,16,5120]{2,1,0:T(8,128)(2,1)}), bf16[32,16,5120]{2,1,0:T(8,128)(2,1)}) %all-gather.2.cloned.1.call-update) | async-done | bytes 5242896 | tf_op jit(solution)/shard_map/all_gather | solution.py:83
  85.4 5.7 %gather_fusion.1 = bf16[32,16,5120]{2,1,0:T(8,128)(2,1)} fusion(bf16[32,16,5120]{2,1,0:T(8,128)(2,1)} %all-gather.2.cloned.1.call-done, s32[1024]{0:T(1024)S(1)} %pad_clamp_fusion), kind=kCustom, calls=%fused_computation.7 | custom fusion | bytes 10485888 | tf_op jit(solution)/shard_map/jit(_take)/gather | solution.py:84
  91.1 3.0 %broadcast_select_fusion = bf16[32,16,5120]{2,1,0:T(8,128)(2,1)S(1)} fusion(bf16[32,16,5120]{2,1,0:T(8,128)(2,1)} %gather_fusion.1, pred[32]{0:T(512)(128)(4,1)S(1)} %compare_and_fusion.2), kind=kLoop, calls=%fused_computation.9 | loop fusion | flops 2621440 | bytes 10485792 | tf_op jit(solution)/shard_map/jit(_take)/select_n | solution.py:84
  94.1 1.9 convolution_convert_fusion
  96.1 115.5 %reduce-scatter.2.cloned.1.call-done = bf16[8,5120]{1,0:T(8,128)(2,1)} async-done(((bf16[128,5120]{1,0:T(8,128)(2,1)}), bf16[8,5120]{1,0:T(8,128)(2,1)}) %reduce-scatter.2.cloned.1.call-update) | async-done | bytes 81936 | tf_op jit(solution)/shard_map/reduce_scatter | solution.py:85
  (32 shorter events, 3.1 us)
Async XLA Ops:
  6.5 14.3 %copy-start = (bf16[32,4,512]{2,1,0:T(4,128)(2,1)S(1)}, bf16[32,4,512]{2,1,0:T(4,128)(2,1)}, u32[]{:S(2)}) copy-start(bf16[32,4,512]{2,1,0:T(4,128)(2,1)} %param.14) | copy-start | bytes 393220
  6.5 47.6 %copy-start.1 = (bf16[32,128,128]{2,1,0:T(8,128)(2,1)S(1)}, bf16[32,128,128]{2,1,0:T(8,128)(2,1)}, u32[]{:S(2)}) copy-start(bf16[32,128,128]{2,1,0:T(8,128)(2,1)} %param.17) | copy-start | bytes 3145732
  6.5 78.8 %all-gather.2.cloned.1.call-start = ((), (), s32[]{:S(2)}) async-start(), calls=%async_computation.4 | async-start | bytes 5406720 | tf_op jit(solution)/shard_map/all_gather | solution.py:83
  11.6 15.0 %all-to-all-start.1 = ((bf16[32,4,128]{2,1,0:T(4,128)(2,1)}), bf16[32,4,128]{2,1,0:T(4,128)(2,1)S(1)}, u32[]{:S(2)}, u32[]{:S(2)}) async-start(bf16[32,4,128]{2,1,0:T(4,128)(2,1)} %get-tuple-element.24), calls=%async_computation.1 | async-start | bytes 65536 | tf_op jit(solution)/shard_map/all_to_all | solution.py:69
  26.6 13.4 %all-to-all-start = ((bf16[32,4,128]{2,1,0:T(4,128)(2,1)}), bf16[32,4,128]{2,1,0:T(4,128)(2,1)S(1)}, u32[]{:S(2)}, u32[]{:S(2)}) async-start(bf16[32,4,128]{2,1,0:T(4,128)(2,1)} %get-tuple-element.25), calls=%async_computation | async-start | bytes 65536 | tf_op jit(solution)/shard_map/all_to_all | solution.py:70
  40.1 13.2 %all-to-all-start.2 = ((bf16[32,4,512]{2,1,0:T(4,128)(2,1)}), bf16[32,4,512]{2,1,0:T(4,128)(2,1)S(1)}, u32[]{:S(2)}, u32[]{:S(2)}) async-start(bf16[32,4,512]{2,1,0:T(4,128)(2,1)} %broadcast_select_fusion.2), calls=%async_computation.2 | async-start | bytes 262144 | tf_op jit(solution)/shard_map/all_to_all | solution.py:68
  46.0 165.6 %reduce-scatter.2.cloned.1.call-start = ((), (), s32[]{:S(2)}) async-start(), calls=%async_computation.5 | async-start | bytes 1392640 | tf_op jit(solution)/shard_map/reduce_scatter | solution.py:85
  54.2 1.8 copy-start.2
Sparse Core Ops, SparseCore 0:
  9.5 75.8 all-gather.1
  96.2 115.3 reduce-scatter.1
where the time goes:
time: 219 us; the launch traced here: 218 us
  waiting for transfers between devices  157 us (72%)
  starting transfers between devices  23 us (11%)
  between operations  13.6 us (6%)
  local copies, waits for them, and re-layouts  12.5 us (6%)
  other arithmetic  9.42 us (4%)
  matrix products  3.29 us (2%)
    reduce_scatter x1, waiting for transfers between devices, on_device(): lax.psum_scatter(jnp.dot(flat_rows, w_slice, preferred_element_type=jnp.f...  116 us
    all_gather x1, waiting for transfers between devices, on_device(): gathered = lax.all_gather(new_wo, 'replica', axis=0, tiled=True)  28.9 us
    all_to_all x1, starting transfers between devices, on_device(): lax.all_to_all(outgoing[1], 'replica', split_axis=0, concat_axis=0, tiled...  9.23 us
    all_to_all x1, starting transfers between devices, on_device(): lax.all_to_all(outgoing[2], 'replica', split_axis=0, concat_axis=0, tiled...  7.82 us
    all_to_all x1, starting transfers between devices, on_device(): lax.all_to_all(outgoing[0], 'replica', split_axis=0, concat_axis=0, tiled...  5.94 us
    all_to_all x1, waiting for transfers between devices, on_device(): lax.all_to_all(outgoing[0], 'replica', split_axis=0, concat_axis=0, tiled...  5.83 us
    gather x1, local copies, waits for them, and re-layouts, on_device(): w_slice = jnp.take(gathered, owner_map, axis=0).reshape(-1, out_width)  5.71 us
    all_to_all x1, waiting for transfers between devices, on_device(): lax.all_to_all(outgoing[2], 'replica', split_axis=0, concat_axis=0, tiled...  5.59 us
  transfers between devices with their start and end apart: 5, of which 4 were waited for; matrix products, arithmetic and copies ran while one was open for 7% of the time, Pallas kernels for 0%

commit v1 on v0

v1 whole, which is shorter than its diff:
```python
import functools
import math

import jax
import jax.numpy as jnp
from jax import lax
from jax.experimental import pallas as pl
from jax.experimental.pallas import tpu as pltpu
from jax.sharding import Mesh
from jax.sharding import PartitionSpec as P

HD = 128
TURN = 4
HEADS = 4
OWN = 16
REPL = ("z_lo", "y", "core")
TENS = ("z_hi", "x")
NREP = 32
NCOL = 8
SLOTS = 32
QROWS = HEADS * TURN
VM = pl.BlockSpec(memory_space=pltpu.VMEM)
SM = pl.BlockSpec(memory_space=pltpu.SMEM)


def pack_kernel(index_ref, q_ref, k_ref, v_ref, w_ref, out_ref):
    blocks = w_ref.shape[2] // NCOL // HD
    for part in range(NCOL):
        for j in range(blocks):
            first = (part * blocks + j) * HD
            piece = w_ref[0, :, first : first + HD]
            for far in range(NREP // NCOL):
                out_ref[far * NCOL + part, j * OWN : (j + 1) * OWN, :] = piece
    base = blocks * OWN
    for r in range(NREP):
        i = index_ref[r]
        rows = q_ref[i]
        for h in range(HEADS):
            out_ref[r, base + h * TURN : base + (h + 1) * TURN, :] = rows[:, h * HD : (h + 1) * HD]
        out_ref[r, base + QROWS : base + QROWS + TURN, :] = k_ref[i]
        out_ref[r, base + QROWS + TURN : base + QROWS + 2 * TURN, :] = v_ref[i]


def attend_kernel(base, own_ref, serve_ref, turn_ref, cache_ref, got_ref, ck_ref, cv_ref, out_ref, nk, nv, s1, acc):
    own = own_ref[0]
    rows = SLOTS * QROWS
    scale = 1.0 / math.sqrt(HD)
    lane = lax.broadcasted_iota(jnp.int32, (QROWS, HD), 1)
    turn_pos = lax.broadcasted_iota(jnp.int32, (QROWS, HD), 0) % TURN
    queries = []
    for s in range(SLOTS):
        source = serve_ref[own, s] // NREP
        queries.append(got_ref[source, base : base + QROWS, :])
        nk[s * TURN : (s + 1) * TURN, :] = got_ref[source, base + QROWS : base + QROWS + TURN, :]
        nv[s * TURN : (s + 1) * TURN, :] = got_ref[source, base + QROWS + TURN : base + QROWS + 2 * TURN, :]
        raw = lax.dot_general(queries[s], ck_ref[s], (((1,), (1,)), ((), ())), preferred_element_type=jnp.float32)
        s1[s * QROWS : (s + 1) * QROWS, :] = jnp.where(lane < cache_ref[s], raw * scale, -jnp.inf)
    all_q = jnp.concatenate(queries, axis=0)
    fresh = lax.dot_general(all_q, nk[...], (((1,), (1,)), ((), ())), preferred_element_type=jnp.float32)
    row = lax.broadcasted_iota(jnp.int32, (rows, SLOTS * TURN), 0)
    col = lax.broadcasted_iota(jnp.int32, (rows, SLOTS * TURN), 1)
    seen = (col // TURN == row // QROWS) & (col % TURN <= row % TURN)
    fresh = jnp.where(seen, fresh * scale, -jnp.inf)
    cached = s1[...]
    top = jnp.max(jnp.maximum(cached, fresh), axis=1, keepdims=True)
    e1 = jnp.exp(cached - top)
    e2 = jnp.exp(fresh - top)
    total = jnp.sum(e1 + e2, axis=1, keepdims=True)
    w1 = (e1 / total).astype(jnp.bfloat16)
    w2 = (e2 / total).astype(jnp.bfloat16)
    acc[...] = jnp.dot(w2, nv[...], preferred_element_type=jnp.float32)
    for s in range(SLOTS):
        part = slice(s * QROWS, (s + 1) * QROWS)
        mixed = acc[part, :] + jnp.dot(w1[part, :], cv_ref[s], preferred_element_type=jnp.float32)
        live = turn_ref[serve_ref[own, s]]
        mixed = jnp.where(turn_pos < live, mixed, 0.0).astype(jnp.bfloat16)
        t = s // 2
        z, x, at = t // 4, t % 4, (s % 2) * TURN
        for h in range(HEADS):
            out_ref[x, z, at : at + TURN, h * HD : (h + 1) * HD] = mixed[h * TURN : (h + 1) * TURN, :]


def weight_kernel(owner_ref, got_ref, out_ref):
    for b in range(NREP):
        source = owner_ref[b]
        for j in range(out_ref.shape[1] // HD):
            out_ref[b * OWN : (b + 1) * OWN, j * HD : (j + 1) * HD] = got_ref[source, j * OWN : (j + 1) * OWN, :]


def matmul_kernel(rows_ref, w_ref, out_ref):
    for x in range(out_ref.shape[0]):
        block = rows_ref[:, x].reshape(out_ref.shape[1], rows_ref.shape[-1])
        out_ref[x] = jnp.dot(block, w_ref[...], preferred_element_type=jnp.float32).astype(jnp.bfloat16)


def on_device(
    queries,
    new_keys,
    new_values,
    cache_keys,
    cache_values,
    serve_lists,
    turn_lens,
    cache_lens,
    owner_map,
    new_wo,
):
    own = lax.axis_index(REPL)
    out_width = new_wo.shape[2]
    width = out_width // NCOL
    base = width // HD * OWN
    sources = serve_lists // NREP
    send_index = jnp.sum(jnp.where(sources == own, serve_lists % NREP, 0), axis=1)
    packed = pl.pallas_call(
        pack_kernel,
        out_shape=jax.ShapeDtypeStruct((NREP, base + QROWS + 2 * TURN, HD), jnp.bfloat16),
        in_specs=[SM, VM, VM, VM, VM],
        out_specs=VM,
    )(send_index, queries, new_keys, new_values, new_wo)
    got = lax.all_to_all(packed, REPL, split_axis=0, concat_axis=0, tiled=True)
    attended = pl.pallas_call(
        functools.partial(attend_kernel, base),
        out_shape=jax.ShapeDtypeStruct((4, 4, 2 * TURN, HEADS * HD), jnp.bfloat16),
        in_specs=[SM, SM, SM, SM, VM, VM, VM],
        out_specs=VM,
        scratch_shapes=[
            pltpu.VMEM((SLOTS * TURN, HD), jnp.bfloat16),
            pltpu.VMEM((SLOTS * TURN, HD), jnp.bfloat16),
            pltpu.VMEM((SLOTS * QROWS, HD), jnp.float32),
            pltpu.VMEM((SLOTS * QROWS, HD), jnp.float32),
        ],
    )(own.reshape(1), serve_lists, turn_lens, cache_lens, got, cache_keys, cache_values)
    copies = jnp.broadcast_to(attended[None], (NCOL,) + attended.shape)
    rows = lax.all_to_all(copies, ("y", "core"), split_axis=0, concat_axis=0, tiled=True)
    weight = pl.pallas_call(
        weight_kernel,
        out_shape=jax.ShapeDtypeStruct((NREP * OWN, width), jnp.bfloat16),
        in_specs=[SM, VM],
        out_specs=VM,
        cost_estimate=pl.CostEstimate(flops=0, bytes_accessed=2 * 2 * NREP * OWN * width, transcendentals=0),
    )(owner_map, got)
    partial = pl.pallas_call(
        matmul_kernel,
        out_shape=jax.ShapeDtypeStruct((4, NCOL * 4 * 2 * TURN, width), jnp.bfloat16),
        in_specs=[VM, VM],
        out_specs=VM,
    )(rows, weight)
    over_x = lax.all_to_all(partial, "x", split_axis=0, concat_axis=0, tiled=True)
    summed = jnp.sum(over_x.astype(jnp.float32), axis=0).astype(jnp.bfloat16)
    summed = summed.reshape(NCOL * 4, 2 * TURN, width)
    over_z = lax.all_to_all(summed, ("y", "core", "z_hi"), split_axis=0, concat_axis=0, tiled=True)
    over_z = over_z.reshape(NCOL, 4, 2 * TURN, width)
    projected = jnp.sum(over_z.astype(jnp.float32), axis=1).astype(jnp.bfloat16)
    return jnp.transpose(projected, (1, 0, 2)).reshape(1, 2 * TURN, out_width)


def solution(mesh):
    fine = Mesh(mesh.devices.reshape(4, 4, 2, 4, 4), REPL + TENS)
    placed = (
        P(REPL, None, TENS),
        P(REPL, None, TENS),
        P(REPL, None, TENS),
        P(REPL, None, TENS),
        P(REPL, None, TENS),
        P(),
        P(),
        P(REPL),
        P(),
        P(REPL, TENS, None),
    )
    return jax.shard_map(
        on_device,
        mesh=fine,
        in_specs=placed,
        out_specs=P(REPL, TENS, None),
        check_vma=False,
    )
```

time: 219 us -> 128 us (0.58)
  the two profiles are of different devices: /device:TPU:16 before, /device:TPU:33 now
where the time goes in v1:
time: 128 us; the launch traced here: 127 us
  blocking collectives  94.5 us (74%)
  waiting for transfers between devices  12.4 us (10%)
  Pallas kernels  11.5 us (9%)
  starting transfers between devices  3.51 us (3%)
  local copies, waits for them, and re-layouts  3 us (2%)
  other arithmetic  2.38 us (2%)
    all_to_all x1, blocking collectives, on_device(): lax.all_to_all(summed, ('y', 'core', 'z_hi'), split_axis=0, concat_axis=0...  41.2 us
    all_to_all x1, blocking collectives, on_device(): got = lax.all_to_all(packed, REPL, split_axis=0, concat_axis=0, tiled=True)  32.8 us
    all_to_all x1, blocking collectives, on_device(): lax.all_to_all(partial, 'x', split_axis=0, concat_axis=0, tiled=True)  20.5 us
    all_to_all x1, waiting for transfers between devices, on_device(): lax.all_to_all(copies, ('y', 'core'), split_axis=0, concat_axis=0, tiled=...  12.4 us
    pallas_call x1, Pallas kernels, on_device(): pl.pallas_call(functools.partial(attend_kernel, base), out_shape=jax.Shap...  3.82 us
    all_to_all x1, starting transfers between devices, on_device(): lax.all_to_all(copies, ('y', 'core'), split_axis=0, concat_axis=0, tiled=...  3.51 us
    pallas_call x1, Pallas kernels, on_device(): pl.pallas_call(matmul_kernel, out_shape=jax.ShapeDtypeStruct((4, NCOL * 4...  3.45 us
  transfers between devices with their start and end apart: 1, of which 1 were waited for; matrix products, arithmetic and copies ran while one was open for 0% of the time, Pallas kernels for 2%

profile of v1, /device:TPU:33, one launch (start us, length us, event | category | flops | bytes accessed | tf_op | source)
XLA Modules:
  0.0 127.3 jit_solution(4756489790776010786)
XLA Ops:
  0.0 1.4 %fusion.2.index_ref = s32[32]{0:T(128)} fusion(s32[32,32]{1,0:T(8,128)} %serve_ref.1, s32[]{:T(128)} %add.14), kind=kLoop, calls=%fused_computation.8 | loop fusion | flops 22496 | bytes 4228 | tf_op jit(solution)/shard_map/reduce_sum | solution.py:113
  1.4 2.1 %shard_map.100 = bf16[32,104,128]{2,1,0:T(8,128)(2,1)} custom-call(s32[32]{0:T(128)} %fusion.2.index_ref, bf16[32,4,512]{2,1,0:T(4,128)(2,1)} %q_ref.1, bf16[32,4,128]{2,1,0:T(4,128)(2,1)} %k_ref.1, bf16[32,4,128]{2,1,0:T(4,128)(2,1)} %v_ref.1, bf16[1,16,5120]{2,1,0:T(8,128)(2,1)} %w_ref.1), custom_call_target="tpu_custom_call" | custom-call | tf_op jit(solution)/shard_map/pallas_call | solution.py:114
  3.5 32.8 %all_to_all.20.got_ref = bf16[32,104,128]{2,1,0:T(8,128)(2,1)} all-to-all(bf16[32,104,128]{2,1,0:T(8,128)(2,1)} %shard_map.100), channel_id=1, replica_groups=mesh['z_lo'=4,'y'=4,'core'=2,'z_hi'=4,'x'=4] {'z_lo','y','core'}, dimensions={0} | all-to-all | bytes 1703936 | tf_op jit(solution)/shard_map/all_to_all | solution.py:120
  36.3 3.8 %shard_map.101 = bf16[4,4,8,512]{3,2,1,0:T(8,128)(2,1)} custom-call(s32[1]{0:T(128)} %bitcast.own_ref, s32[32,32]{1,0:T(8,128)} %serve_ref.1, s32[1024]{0:T(1024)} %turn_ref.1, s32[32]{0:T(128)} %cache_ref.1, bf16[32,104,128]{2,1,0:T(8,128)(2,1)} %all_to_all.20.got_ref, bf16[32,128,128]{2,1,0:T(8,128)(2,1)} %ck_ref.1, bf16[32,128,128]{2,1,0:T(8,128)(2,1)} %cv_ref.1), custom_call_target="tpu_custom_call" | custom-call | tf_op jit(solution)/shard_map/pallas_call | solution.py:121
  40.1 2.0 %broadcast_in_dim.4 = bf16[8,4,4,8,512]{4,3,2,1,0:T(8,128)(2,1)} broadcast(bf16[4,4,8,512]{3,2,1,0:T(8,128)(2,1)} %shard_map.101), dimensions={1,2,3,4} | broadcast | bytes 1179648 | tf_op jit(solution)/shard_map/broadcast_in_dim | solution.py:133
  42.1 3.5 %all-to-all-start.1 = ((bf16[8,4,4,8,512]{4,3,2,1,0:T(8,128)(2,1)}), bf16[8,4,4,8,512]{4,3,2,1,0:T(8,128)(2,1)S(1)}, u32[]{:S(2)}, u32[]{:S(2)}) async-start(bf16[8,4,4,8,512]{4,3,2,1,0:T(8,128)(2,1)} %broadcast_in_dim.4), calls=%async_computation.1 | async-start | bytes 2097152 | tf_op jit(solution)/shard_map/all_to_all | solution.py:134
  45.7 2.1 %shard_map.102.w_ref = bf16[512,640]{1,0:T(8,128)(2,1)} custom-call(s32[32]{0:T(128)} %owner_ref.1, bf16[32,104,128]{2,1,0:T(8,128)(2,1)} %all_to_all.20.got_ref), custom_call_target="tpu_custom_call" | custom-call | bytes 1310720 | tf_op jit(solution)/shard_map/pallas_call | solution.py:135
  47.8 12.4 %all-to-all-done.1.rows_ref = bf16[8,4,4,8,512]{4,3,2,1,0:T(8,128)(2,1)S(1)} async-done(((bf16[8,4,4,8,512]{4,3,2,1,0:T(8,128)(2,1)}), bf16[8,4,4,8,512]{4,3,2,1,0:T(8,128)(2,1)S(1)}, u32[]{:S(2)}, u32[]{:S(2)}) %all-to-all-start.1) | async-done | bytes 1048608 | tf_op jit(solution)/shard_map/all_to_all | solution.py:134
  60.1 0.0 copy-start
  60.1 1.0 copy-done
  61.1 3.5 %shard_map.103 = bf16[4,256,640]{2,1,0:T(8,128)(2,1)} custom-call(bf16[8,4,4,8,512]{4,3,2,1,0:T(8,128)(2,1)} %copy-done, bf16[512,640]{1,0:T(8,128)(2,1)} %shard_map.102.w_ref), custom_call_target="tpu_custom_call" | custom-call | tf_op jit(solution)/shard_map/pallas_call | solution.py:142
  64.6 20.5 %all_to_all.21 = bf16[4,256,640]{2,1,0:T(8,128)(2,1)S(1)} all-to-all(bf16[4,256,640]{2,1,0:T(8,128)(2,1)} %shard_map.103), channel_id=1, replica_groups=mesh['z_lo'=4,'y'=4,'core'=2,'z_hi'=4,'x'=4] {'x'}, dimensions={0} | all-to-all | bytes 2621440 | tf_op jit(solution)/shard_map/all_to_all | solution.py:148
  85.1 0.3 reduce_sum.34
  85.4 41.2 %all_to_all.22 = bf16[32,8,640]{2,1,0:T(8,128)(2,1)S(1)} all-to-all(bf16[32,8,640]{2,1,0:T(8,128)(2,1)S(1)} %bitcast.7), channel_id=1, replica_groups=mesh['z_lo'=4,'y'=4,'core'=2,'z_hi'=4,'x'=4] {'y','core','z_hi'}, dimensions={0} | all-to-all | bytes 655360 | tf_op jit(solution)/shard_map/all_to_all | solution.py:151
  126.6 0.7 bitcast_reduce_fusion
Async XLA Ops:
  42.1 18.0 %all-to-all-start.1 = ((bf16[8,4,4,8,512]{4,3,2,1,0:T(8,128)(2,1)}), bf16[8,4,4,8,512]{4,3,2,1,0:T(8,128)(2,1)S(1)}, u32[]{:S(2)}, u32[]{:S(2)}) async-start(bf16[8,4,4,8,512]{4,3,2,1,0:T(8,128)(2,1)} %broadcast_in_dim.4), calls=%async_computation.1 | async-start | bytes 2097152 | tf_op jit(solution)/shard_map/all_to_all | solution.py:134
  60.1 1.0 copy-start

commit v2 on v1

--- a/solution.py
+++ b/solution.py
@@ -1,4 +1,3 @@
-import functools
 import math
 
 import jax
@@ -21,9 +20,20 @@
 QROWS = HEADS * TURN
 VM = pl.BlockSpec(memory_space=pltpu.VMEM)
 SM = pl.BlockSpec(memory_space=pltpu.SMEM)
-
-
-def pack_kernel(index_ref, q_ref, k_ref, v_ref, w_ref, out_ref):
+ROOM = pltpu.CompilerParams(vmem_limit_bytes=16 << 20)
+
+
+def route_kernel(index_ref, q_ref, k_ref, v_ref, out_ref):
+    for r in range(NREP):
+        i = index_ref[r]
+        rows = q_ref[i]
+        for h in range(HEADS):
+            out_ref[r, h * TURN : (h + 1) * TURN, :] = rows[:, h * HD : (h + 1) * HD]
+        out_ref[r, QROWS : QROWS + TURN, :] = k_ref[i]
+        out_ref[r, QROWS + TURN : QROWS + 2 * TURN, :] = v_ref[i]
+
+
+def spread_kernel(w_ref, out_ref):
     blocks = w_ref.shape[2] // NCOL // HD
     for part in range(NCOL):
         for j in range(blocks):
@@ -31,17 +41,9 @@
             piece = w_ref[0, :, first : first + HD]
             for far in range(NREP // NCOL):
                 out_ref[far * NCOL + part, j * OWN : (j + 1) * OWN, :] = piece
-    base = blocks * OWN
-    for r in range(NREP):
-        i = index_ref[r]
-        rows = q_ref[i]
-        for h in range(HEADS):
-            out_ref[r, base + h * TURN : base + (h + 1) * TURN, :] = rows[:, h * HD : (h + 1) * HD]
-        out_ref[r, base + QROWS : base + QROWS + TURN, :] = k_ref[i]
-        out_ref[r, base + QROWS + TURN : base + QROWS + 2 * TURN, :] = v_ref[i]
-
-
-def attend_kernel(base, own_ref, serve_ref, turn_ref, cache_ref, got_ref, ck_ref, cv_ref, out_ref, nk, nv, s1, acc):
+
+
+def attend_kernel(own_ref, serve_ref, turn_ref, cache_ref, got_ref, ck_ref, cv_ref, out_ref, nk, nv, s1, acc):
     own = own_ref[0]
     rows = SLOTS * QROWS
     scale = 1.0 / math.sqrt(HD)
@@ -50,9 +52,9 @@
     queries = []
     for s in range(SLOTS):
         source = serve_ref[own, s] // NREP
-        queries.append(got_ref[source, base : base + QROWS, :])
-        nk[s * TURN : (s + 1) * TURN, :] = got_ref[source, base + QROWS : base + QROWS + TURN, :]
-        nv[s * TURN : (s + 1) * TURN, :] = got_ref[source, base + QROWS + TURN : base + QROWS + 2 * TURN, :]
+        queries.append(got_ref[source, 0:QROWS, :])
+        nk[s * TURN : (s + 1) * TURN, :] = got_ref[source, QROWS : QROWS + TURN, :]
+        nv[s * TURN : (s + 1) * TURN, :] = got_ref[source, QROWS + TURN : QROWS + 2 * TURN, :]
         raw = lax.dot_general(queries[s], ck_ref[s], (((1,), (1,)), ((), ())), preferred_element_type=jnp.float32)
         s1[s * QROWS : (s + 1) * QROWS, :] = jnp.where(lane < cache_ref[s], raw * scale, -jnp.inf)
     all_q = jnp.concatenate(queries, axis=0)
@@ -87,10 +89,13 @@
             out_ref[b * OWN : (b + 1) * OWN, j * HD : (j + 1) * HD] = got_ref[source, j * OWN : (j + 1) * OWN, :]
 
 
-def matmul_kernel(rows_ref, w_ref, out_ref):
-    for x in range(out_ref.shape[0]):
-        block = rows_ref[:, x].reshape(out_ref.shape[1], rows_ref.shape[-1])
-        out_ref[x] = jnp.dot(block, w_ref[...], preferred_element_type=jnp.float32).astype(jnp.bfloat16)
+def matmul_kernel(core_ref, near_ref, far_ref, w_ref, out_ref, rows):
+    core = core_ref[0]
+    for y in range(4):
+        rows[y, core] = near_ref[y, 0]
+        rows[y, 1 - core] = far_ref[y, 0]
+    block = rows[...].reshape(out_ref.shape[1], rows.shape[-1])
+    out_ref[0] = jnp.dot(block, w_ref[...], preferred_element_type=jnp.float32).astype(jnp.bfloat16)
 
 
 def on_device(
@@ -108,19 +113,29 @@
     own = lax.axis_index(REPL)
     out_width = new_wo.shape[2]
     width = out_width // NCOL
-    base = width // HD * OWN
     sources = serve_lists // NREP
     send_index = jnp.sum(jnp.where(sources == own, serve_lists % NREP, 0), axis=1)
-    packed = pl.pallas_call(
-        pack_kernel,
-        out_shape=jax.ShapeDtypeStruct((NREP, base + QROWS + 2 * TURN, HD), jnp.bfloat16),
-        in_specs=[SM, VM, VM, VM, VM],
-        out_specs=VM,
-    )(send_index, queries, new_keys, new_values, new_wo)
-    got = lax.all_to_all(packed, REPL, split_axis=0, concat_axis=0, tiled=True)
+    routed = pl.pallas_call(
+        route_kernel,
+        out_shape=jax.ShapeDtypeStruct((NREP, QROWS + 2 * TURN, HD), jnp.bfloat16),
+        compiler_params=ROOM,
+        in_specs=[SM, VM, VM, VM],
+        out_specs=VM,
+    )(send_index, queries, new_keys, new_values)
+    spread = pl.pallas_call(
+        spread_kernel,
+        out_shape=jax.ShapeDtypeStruct((NREP, width // HD * OWN, HD), jnp.bfloat16),
+        compiler_params=ROOM,
+        in_specs=[VM],
+        out_specs=VM,
+    )(new_wo)
+    got = lax.all_to_all(routed, REPL, split_axis=0, concat_axis=0, tiled=True)
+    got, spread = lax.optimization_barrier((got, spread))
+    pieces = lax.all_to_all(spread, REPL, split_axis=0, concat_axis=0, tiled=True)
     attended = pl.pallas_call(
-        functools.partial(attend_kernel, base),
+        attend_kernel,
         out_shape=jax.ShapeDtypeStruct((4, 4, 2 * TURN, HEADS * HD), jnp.bfloat16),
+        compiler_params=ROOM,
         in_specs=[SM, SM, SM, SM, VM, VM, VM],
         out_specs=VM,
         scratch_shapes=[
@@ -129,22 +144,33 @@
             pltpu.VMEM((SLOTS * QROWS, HD), jnp.float32),
             pltpu.VMEM((SLOTS * QROWS, HD), jnp.float32),
         ],
+        cost_estimate=pl.CostEstimate(flops=1 << 30, bytes_accessed=8 << 20, transcendentals=1 << 17),
     )(own.reshape(1), serve_lists, turn_lens, cache_lens, got, cache_keys, cache_values)
-    copies = jnp.broadcast_to(attended[None], (NCOL,) + attended.shape)
-    rows = lax.all_to_all(copies, ("y", "core"), split_axis=0, concat_axis=0, tiled=True)
+    near = lax.all_gather(attended, "y", axis=0)
+    far = lax.ppermute(near, "core", [(0, 1), (1, 0)])
     weight = pl.pallas_call(
         weight_kernel,
         out_shape=jax.ShapeDtypeStruct((NREP * OWN, width), jnp.bfloat16),
+        compiler_params=ROOM,
         in_specs=[SM, VM],
         out_specs=VM,
         cost_estimate=pl.CostEstimate(flops=0, bytes_accessed=2 * 2 * NREP * OWN * width, transcendentals=0),
-    )(owner_map, got)
+    )(owner_map, pieces)
+    block = (4, 1, 4, 2 * TURN, HEADS * HD)
     partial = pl.pallas_call(
         matmul_kernel,
         out_shape=jax.ShapeDtypeStruct((4, NCOL * 4 * 2 * TURN, width), jnp.bfloat16),
-        in_specs=[VM, VM],
-        out_specs=VM,
-    )(rows, weight)
+        grid=(4,),
+        compiler_params=ROOM,
+        in_specs=[
+            SM,
+            pl.BlockSpec(block, lambda x: (0, x, 0, 0, 0)),
+            pl.BlockSpec(block, lambda x: (0, x, 0, 0, 0)),
+            pl.BlockSpec((NREP * OWN, width), lambda x: (0, 0)),
+        ],
+        out_specs=pl.BlockSpec((1, NCOL * 4 * 2 * TURN, width), lambda x: (x, 0, 0)),
+        scratch_shapes=[pltpu.VMEM((4, 2, 4, 2 * TURN, HEADS * HD), jnp.bfloat16)],
+    )(lax.axis_index("core").reshape(1), near, far, weight)
     over_x = lax.all_to_all(partial, "x", split_axis=0, concat_axis=0, tiled=True)
     summed = jnp.sum(over_x.astype(jnp.float32), axis=0).astype(jnp.bfloat16)
     summed = summed.reshape(NCOL * 4, 2 * TURN, width)

time: 128 us -> 115 us (0.90)
  the two profiles are of different devices: /device:TPU:33 before, /device:TPU:65 now
where the time goes in v2:
time: 115 us; the launch traced here: 114 us
  blocking collectives  74.8 us (65%)
  starting transfers between devices  19.4 us (17%)
  waiting for transfers between devices  6.78 us (6%)
  Pallas kernels  6.73 us (6%)
  local copies, waits for them, and re-layouts  4.57 us (4%)
  other arithmetic  1.85 us (2%)
    all_to_all x1, blocking collectives, on_device(): lax.all_to_all(summed, ('y', 'core', 'z_hi'), split_axis=0, concat_axis=0...  42 us
    all_to_all x1, blocking collectives, on_device(): lax.all_to_all(partial, 'x', split_axis=0, concat_axis=0, tiled=True)  20.6 us
    all_gather x1, blocking collectives, on_device(): near = lax.all_gather(attended, 'y', axis=0)  12.2 us
    all_to_all x1, starting transfers between devices, on_device(): got = lax.all_to_all(routed, REPL, split_axis=0, concat_axis=0, tiled=True)  9.09 us
    all_to_all x1, waiting for transfers between devices, on_device(): got = lax.all_to_all(routed, REPL, split_axis=0, concat_axis=0, tiled=True)  5.96 us
    all_to_all x1, starting transfers between devices, on_device(): lax.all_to_all(spread, REPL, split_axis=0, concat_axis=0, tiled=True)  5.8 us
    unnamed x20, local copies, waits for them, and re-layouts  4.57 us
    ppermute x1, starting transfers between devices, on_device(): far = lax.ppermute(near, 'core', [(0, 1), (1, 0)])  4.52 us
  transfers between devices with their start and end apart: 3, of which 2 were waited for; matrix products, arithmetic and copies ran while one was open for 0% of the time, Pallas kernels for 3%

profile of v2, /device:TPU:65, one launch (start us, length us, event | category | flops | bytes accessed | tf_op | source)
XLA Modules:
  0.0 114.3 jit_solution(10569066238998023495)
XLA Ops:
  0.0 0.8 fusion.2.index_ref
  0.9 0.9 copy-done.1
  1.8 0.8 copy-done.2
  2.5 0.8 copy-done.3
  3.3 1.3 %shard_map.100 = bf16[32,24,128]{2,1,0:T(8,128)(2,1)} custom-call(s32[32]{0:T(128)S(1)} %fusion.2.index_ref, bf16[32,4,512]{2,1,0:T(4,128)(2,1)S(1)} %copy-done.1, bf16[32,4,128]{2,1,0:T(4,128)(2,1)S(1)} %copy-done.2, bf16[32,4,128]{2,1,0:T(4,128)(2,1)S(1)} %copy-done.3), custom_call_target="tpu_custom_call" | custom-call | tf_op jit(solution)/shard_map/pallas_call | solution.py:118
  4.6 9.1 %all-to-all-start = ((bf16[32,24,128]{2,1,0:T(8,128)(2,1)}), bf16[32,24,128]{2,1,0:T(8,128)(2,1)S(1)}, u32[]{:S(2)}, u32[]{:S(2)}) async-start(bf16[32,24,128]{2,1,0:T(8,128)(2,1)} %shard_map.100), calls=%async_computation | async-start | bytes 393216 | tf_op jit(solution)/shard_map/all_to_all | solution.py:132
  13.7 0.0 copy-start
  13.7 0.9 copy-done
  14.6 0.9 shard_map.101
  15.5 6.0 %all-to-all-done.got_ref = bf16[32,24,128]{2,1,0:T(8,128)(2,1)S(1)} async-done(((bf16[32,24,128]{2,1,0:T(8,128)(2,1)}), bf16[32,24,128]{2,1,0:T(8,128)(2,1)S(1)}, u32[]{:S(2)}, u32[]{:S(2)}) %all-to-all-start) | async-done | bytes 196640 | tf_op jit(solution)/shard_map/all_to_all | solution.py:132
  21.5 5.8 %all-to-all-start.1 = ((bf16[32,80,128]{2,1,0:T(8,128)(2,1)}), bf16[32,80,128]{2,1,0:T(8,128)(2,1)S(1)}, u32[]{:S(2)}, u32[]{:S(2)}) async-start(bf16[32,80,128]{2,1,0:T(8,128)(2,1)} %shard_map.101), calls=%async_computation.1 | async-start | bytes 1310720 | tf_op jit(solution)/shard_map/all_to_all | solution.py:134
  27.3 0.0 copy-start.7
  27.4 1.2 %copy-done.7 = bf16[32,128,128]{2,1,0:T(8,128)(2,1)S(1)} copy-done((bf16[32,128,128]{2,1,0:T(8,128)(2,1)S(1)}, bf16[32,128,128]{2,1,0:T(8,128)(2,1)}, u32[]{:S(2)}) %copy-start.7) | copy-done | bytes 1048600
  28.6 2.2 %shard_map.102 = bf16[4,4,8,512]{3,2,1,0:T(8,128)(2,1)S(1)} custom-call(s32[1]{0:T(128)} %bitcast.1.own_ref, s32[32,32]{1,0:T(8,128)S(1)} %copy-done.4, s32[1024]{0:T(1024)S(1)} %copy-done.8, s32[32]{0:T(128)S(1)} %copy-done.9, bf16[32,24,128]{2,1,0:T(8,128)(2,1)S(1)} %all-to-all-done.got_ref, bf16[32,128,128]{2,1,0:T(8,128)(2,1)S(1)} %copy-done.6, ...), custom_call_target="tpu_custom_call" | custom-call | flops 1073741824 | bytes 8388608 | tf_op jit(solution)/shard_map/pallas_call | solution.py:135
  30.8 12.2 %all-gather = bf16[16,4,8,512]{3,2,1,0:T(8,128)(2,1)S(1)} all-gather(bf16[4,4,8,512]{3,2,1,0:T(8,128)(2,1)S(1)} %shard_map.102), channel_id=2, replica_groups=mesh['z_lo'=4,'y'=4,'core'=2,'z_hi'=4,'x'=4] {'y'}, dimensions={0}, use_global_device_ids=true | all-gather | bytes 655360 | tf_op jit(solution)/shard_map/all_gather | solution.py:149
  43.0 4.5 %collective-permute-start = (bf16[4,4,4,8,512]{4,3,2,1,0:T(8,128)(2,1)S(1)}, bf16[4,4,4,8,512]{4,3,2,1,0:T(8,128)(2,1)S(1)}, u32[]{:S(2)}, u32[]{:S(2)}) collective-permute-start(bf16[4,4,4,8,512]{4,3,2,1,0:T(8,128)(2,1)S(1)} %bitcast.9), channel_id=1, source_target_pairs={{0,16},{16,0},{1,17},{17,1},{2,18},{18,2},{3,19},{19,3},{4,20},{20... | collective-permute-start | bytes 1572872 | tf_op jit(solution)/shard_map/ppermute | solution.py:150
  47.5 0.0 all-to-all-done.1.got_ref
  47.5 0.7 shard_map.103.w_ref
  48.2 0.8 collective-permute-done.far_ref
  49.0 1.6 %shard_map.104 = bf16[4,256,640]{2,1,0:T(8,128)(2,1)S(1)} custom-call(s32[1]{0:T(128)} %bitcast.core_ref, bf16[4,4,4,8,512]{4,3,2,1,0:T(8,128)(2,1)S(1)} %bitcast.10, bf16[4,4,4,8,512]{4,3,2,1,0:T(8,128)(2,1)S(1)} %collective-permute-done.far_ref, bf16[512,640]{1,0:T(8,128)(2,1)S(1)} %shard_map.103.w_ref), custom_call_target="tpu_custom_call" | custom-call | tf_op jit(solution)/shard_map/pallas_call | solution.py:160
  50.6 20.6 %all_to_all.20 = bf16[4,256,640]{2,1,0:T(8,128)(2,1)S(1)} all-to-all(bf16[4,256,640]{2,1,0:T(8,128)(2,1)S(1)} %shard_map.104), channel_id=1, replica_groups=mesh['z_lo'=4,'y'=4,'core'=2,'z_hi'=4,'x'=4] {'x'}, dimensions={0} | all-to-all | bytes 2621440 | tf_op jit(solution)/shard_map/all_to_all | solution.py:174
  71.3 0.3 reduce_sum.34
  71.6 42.0 %all_to_all.21 = bf16[32,8,640]{2,1,0:T(8,128)(2,1)S(1)} all-to-all(bf16[32,8,640]{2,1,0:T(8,128)(2,1)S(1)} %bitcast.11), channel_id=1, replica_groups=mesh['z_lo'=4,'y'=4,'core'=2,'z_hi'=4,'x'=4] {'y','core','z_hi'}, dimensions={0} | all-to-all | bytes 655360 | tf_op jit(solution)/shard_map/all_to_all | solution.py:177
  113.6 0.7 bitcast_reduce_fusion
  (13 shorter events, 0.0 us)
Async XLA Ops:
  0.8 0.9 copy-start.1
  1.8 0.8 copy-start.2
  2.5 0.8 copy-start.3
  4.6 22.7 %copy-start.4 = (s32[32,32]{1,0:T(8,128)S(1)}, s32[32,32]{1,0:T(8,128)}, u32[]{:S(2)}) copy-start(s32[32,32]{1,0:T(8,128)} %serve_ref.1) | copy-start | bytes 12292
  4.6 22.7 %copy-start.8 = (s32[1024]{0:T(1024)S(1)}, s32[1024]{0:T(1024)}, u32[]{:S(2)}) copy-start(s32[1024]{0:T(1024)} %turn_ref.1) | copy-start | bytes 12292
  4.6 22.7 %copy-start.9 = (s32[32]{0:T(128)S(1)}, s32[32]{0:T(128)}, u32[]{:S(2)}) copy-start(s32[32]{0:T(128)} %cache_ref.1) | copy-start | bytes 388
  4.6 16.9 %all-to-all-start = ((bf16[32,24,128]{2,1,0:T(8,128)(2,1)}), bf16[32,24,128]{2,1,0:T(8,128)(2,1)S(1)}, u32[]{:S(2)}, u32[]{:S(2)}) async-start(bf16[32,24,128]{2,1,0:T(8,128)(2,1)} %shard_map.100), calls=%async_computation | async-start | bytes 393216 | tf_op jit(solution)/shard_map/all_to_all | solution.py:132
  13.7 0.9 copy-start
  14.6 12.7 %copy-start.6 = (bf16[32,128,128]{2,1,0:T(8,128)(2,1)S(1)}, bf16[32,128,128]{2,1,0:T(8,128)(2,1)}, u32[]{:S(2)}) copy-start(bf16[32,128,128]{2,1,0:T(8,128)(2,1)} %ck_ref.1) | copy-start | bytes 3145732
  21.5 26.0 %all-to-all-start.1 = ((bf16[32,80,128]{2,1,0:T(8,128)(2,1)}), bf16[32,80,128]{2,1,0:T(8,128)(2,1)S(1)}, u32[]{:S(2)}, u32[]{:S(2)}) async-start(bf16[32,80,128]{2,1,0:T(8,128)(2,1)} %shard_map.101), calls=%async_computation.1 | async-start | bytes 1310720 | tf_op jit(solution)/shard_map/all_to_all | solution.py:134
  27.3 1.2 %copy-start.7 = (bf16[32,128,128]{2,1,0:T(8,128)(2,1)S(1)}, bf16[32,128,128]{2,1,0:T(8,128)(2,1)}, u32[]{:S(2)}) copy-start(bf16[32,128,128]{2,1,0:T(8,128)(2,1)} %cv_ref.1) | copy-start | bytes 3145732
  28.6 19.0 %copy-start.5 = (s32[32]{0:T(128)S(1)}, s32[32]{0:T(128)}, u32[]{:S(2)}) copy-start(s32[32]{0:T(128)} %owner_ref.1) | copy-start | bytes 388
  43.0 6.0 %collective-permute-start = (bf16[4,4,4,8,512]{4,3,2,1,0:T(8,128)(2,1)S(1)}, bf16[4,4,4,8,512]{4,3,2,1,0:T(8,128)(2,1)S(1)}, u32[]{:S(2)}, u32[]{:S(2)}) collective-permute-start(bf16[4,4,4,8,512]{4,3,2,1,0:T(8,128)(2,1)S(1)} %bitcast.9), channel_id=1, source_target_pairs={{0,16},{16,0},{1,17},{17,1},{2,18},{18,2},{3,19},{19,3},{4,20},{20... | collective-permute-start | bytes 1572872 | tf_op jit(solution)/shard_map/ppermute | solution.py:150

commit v3 on v2

--- a/solution.py
+++ b/solution.py
@@ -91,11 +91,11 @@
 
 def matmul_kernel(core_ref, near_ref, far_ref, w_ref, out_ref, rows):
     core = core_ref[0]
-    for y in range(4):
-        rows[y, core] = near_ref[y, 0]
-        rows[y, 1 - core] = far_ref[y, 0]
-    block = rows[...].reshape(out_ref.shape[1], rows.shape[-1])
-    out_ref[0] = jnp.dot(block, w_ref[...], preferred_element_type=jnp.float32).astype(jnp.bfloat16)
+    rows[core] = near_ref[0]
+    rows[1 - core] = far_ref[0]
+    block = rows[...].reshape(2 * rows.shape[1], rows.shape[2])
+    product = jnp.dot(block, w_ref[...], preferred_element_type=jnp.float32).astype(jnp.bfloat16)
+    out_ref[0] = product.reshape(out_ref.shape[1:])
 
 
 def on_device(
@@ -118,7 +118,6 @@
     routed = pl.pallas_call(
         route_kernel,
         out_shape=jax.ShapeDtypeStruct((NREP, QROWS + 2 * TURN, HD), jnp.bfloat16),
-        compiler_params=ROOM,
         in_specs=[SM, VM, VM, VM],
         out_specs=VM,
     )(send_index, queries, new_keys, new_values)
@@ -156,27 +155,28 @@
         out_specs=VM,
         cost_estimate=pl.CostEstimate(flops=0, bytes_accessed=2 * 2 * NREP * OWN * width, transcendentals=0),
     )(owner_map, pieces)
-    block = (4, 1, 4, 2 * TURN, HEADS * HD)
+    served = SLOTS * TURN
+    block = pl.BlockSpec((1, served, HEADS * HD), lambda y: (y, 0, 0))
     partial = pl.pallas_call(
         matmul_kernel,
-        out_shape=jax.ShapeDtypeStruct((4, NCOL * 4 * 2 * TURN, width), jnp.bfloat16),
+        out_shape=jax.ShapeDtypeStruct((4, 2, served, width), jnp.bfloat16),
         grid=(4,),
         compiler_params=ROOM,
-        in_specs=[
-            SM,
-            pl.BlockSpec(block, lambda x: (0, x, 0, 0, 0)),
-            pl.BlockSpec(block, lambda x: (0, x, 0, 0, 0)),
-            pl.BlockSpec((NREP * OWN, width), lambda x: (0, 0)),
-        ],
-        out_specs=pl.BlockSpec((1, NCOL * 4 * 2 * TURN, width), lambda x: (x, 0, 0)),
-        scratch_shapes=[pltpu.VMEM((4, 2, 4, 2 * TURN, HEADS * HD), jnp.bfloat16)],
-    )(lax.axis_index("core").reshape(1), near, far, weight)
-    over_x = lax.all_to_all(partial, "x", split_axis=0, concat_axis=0, tiled=True)
-    summed = jnp.sum(over_x.astype(jnp.float32), axis=0).astype(jnp.bfloat16)
-    summed = summed.reshape(NCOL * 4, 2 * TURN, width)
-    over_z = lax.all_to_all(summed, ("y", "core", "z_hi"), split_axis=0, concat_axis=0, tiled=True)
-    over_z = over_z.reshape(NCOL, 4, 2 * TURN, width)
-    projected = jnp.sum(over_z.astype(jnp.float32), axis=1).astype(jnp.bfloat16)
+        in_specs=[SM, block, block, pl.BlockSpec((NREP * OWN, width), lambda y: (0, 0))],
+        out_specs=pl.BlockSpec((1, 2, served, width), lambda y: (y, 0, 0, 0)),
+        scratch_shapes=[pltpu.VMEM((2, served, HEADS * HD), jnp.bfloat16)],
+    )(
+        lax.axis_index("core").reshape(1),
+        near.reshape(4, served, HEADS * HD),
+        far.reshape(4, served, HEADS * HD),
+        weight,
+    )
+    partial = partial.reshape(NREP, NREP, width)
+    over_x = lax.all_to_all(partial, ("y", "core", "x"), split_axis=0, concat_axis=0, tiled=True)
+    summed = jnp.sum(over_x.reshape(NCOL, 4, 4, 2 * TURN, width).astype(jnp.float32), axis=1)
+    summed = jnp.transpose(summed.astype(jnp.bfloat16), (1, 0, 2, 3))
+    over_z = lax.all_to_all(summed, "z_hi", split_axis=0, concat_axis=0, tiled=True)
+    projected = jnp.sum(over_z.astype(jnp.float32), axis=0).astype(jnp.bfloat16)
     return jnp.transpose(projected, (1, 0, 2)).reshape(1, 2 * TURN, out_width)
 
 

time: 115 us -> 114 us (level)
  local copies, waits for them, and re-layouts: 4.57 us -> 2.18 us
    unnamed x20 -> x14, local copies, waits for them, and re-layouts: 4.57 us -> 2.15 us
where the time goes in v3:
time: 114 us; the launch traced here: 113 us
  blocking collectives  75.2 us (66%)
  starting transfers between devices  19.4 us (17%)
  Pallas kernels  7.02 us (6%)
  waiting for transfers between devices  6.78 us (6%)
  other arithmetic  2.31 us (2%)
  local copies, waits for them, and re-layouts  2.18 us (2%)
    all_to_all x1, blocking collectives, on_device(): lax.all_to_all(summed, 'z_hi', split_axis=0, concat_axis=0, tiled=True)  36.3 us
    all_to_all x1, blocking collectives, on_device(): lax.all_to_all(partial, ('y', 'core', 'x'), split_axis=0, concat_axis=0,...  26.7 us
    all_gather x1, blocking collectives, on_device(): near = lax.all_gather(attended, 'y', axis=0)  12.2 us
    all_to_all x1, starting transfers between devices, on_device(): got = lax.all_to_all(routed, REPL, split_axis=0, concat_axis=0, tiled=True)  9.1 us
    all_to_all x1, waiting for transfers between devices, on_device(): got = lax.all_to_all(routed, REPL, split_axis=0, concat_axis=0, tiled=True)  5.96 us
    all_to_all x1, starting transfers between devices, on_device(): lax.all_to_all(spread, REPL, split_axis=0, concat_axis=0, tiled=True)  5.8 us
    ppermute x1, starting transfers between devices, on_device(): far = lax.ppermute(near, 'core', [(0, 1), (1, 0)])  4.52 us
  transfers between devices with their start and end apart: 3, of which 2 were waited for; matrix products, arithmetic and copies ran while one was open for 0% of the time, Pallas kernels for 3%

profile of v3, /device:TPU:65, one launch (start us, length us, event | category | flops | bytes accessed | tf_op | source)
XLA Modules:
  0.0 113.1 jit_solution(5307012179969099079)
XLA Ops:
  0.0 1.4 %fusion.2.index_ref = s32[32]{0:T(128)} fusion(s32[32,32]{1,0:T(8,128)} %serve_ref.1, s32[]{:T(128)} %add.14), kind=kLoop, calls=%fused_computation.7 | loop fusion | flops 22496 | bytes 4228 | tf_op jit(solution)/shard_map/reduce_sum | solution.py:117
  1.4 1.7 %shard_map.100 = bf16[32,24,128]{2,1,0:T(8,128)(2,1)} custom-call(s32[32]{0:T(128)} %fusion.2.index_ref, bf16[32,4,512]{2,1,0:T(4,128)(2,1)} %q_ref.1, bf16[32,4,128]{2,1,0:T(4,128)(2,1)} %k_ref.1, bf16[32,4,128]{2,1,0:T(4,128)(2,1)} %v_ref.1), custom_call_target="tpu_custom_call" | custom-call | tf_op jit(solution)/shard_map/pallas_call | solution.py:118
  3.1 9.1 %all-to-all-start = ((bf16[32,24,128]{2,1,0:T(8,128)(2,1)}), bf16[32,24,128]{2,1,0:T(8,128)(2,1)S(1)}, u32[]{:S(2)}, u32[]{:S(2)}) async-start(bf16[32,24,128]{2,1,0:T(8,128)(2,1)} %shard_map.100), calls=%async_computation | async-start | bytes 393216 | tf_op jit(solution)/shard_map/all_to_all | solution.py:131
  12.2 0.0 copy-start
  12.2 0.9 copy-done
  13.1 0.9 shard_map.101
  14.1 6.0 %all-to-all-done.got_ref = bf16[32,24,128]{2,1,0:T(8,128)(2,1)S(1)} async-done(((bf16[32,24,128]{2,1,0:T(8,128)(2,1)}), bf16[32,24,128]{2,1,0:T(8,128)(2,1)S(1)}, u32[]{:S(2)}, u32[]{:S(2)}) %all-to-all-start) | async-done | bytes 196640 | tf_op jit(solution)/shard_map/all_to_all | solution.py:131
  20.0 5.8 %all-to-all-start.1 = ((bf16[32,80,128]{2,1,0:T(8,128)(2,1)}), bf16[32,80,128]{2,1,0:T(8,128)(2,1)S(1)}, u32[]{:S(2)}, u32[]{:S(2)}) async-start(bf16[32,80,128]{2,1,0:T(8,128)(2,1)} %shard_map.101), calls=%async_computation.1 | async-start | bytes 1310720 | tf_op jit(solution)/shard_map/all_to_all | solution.py:133
  25.8 0.0 copy-done.1
  25.8 0.0 copy-done.5
  25.8 0.0 copy-done.6
  25.9 0.0 copy-start.4
  25.9 1.2 %copy-done.4 = bf16[32,128,128]{2,1,0:T(8,128)(2,1)S(1)} copy-done((bf16[32,128,128]{2,1,0:T(8,128)(2,1)S(1)}, bf16[32,128,128]{2,1,0:T(8,128)(2,1)}, u32[]{:S(2)}) %copy-start.4) | copy-done | bytes 1048600
  27.1 2.2 %shard_map.102 = bf16[4,4,8,512]{3,2,1,0:T(8,128)(2,1)S(1)} custom-call(s32[1]{0:T(128)} %bitcast.1.own_ref, s32[32,32]{1,0:T(8,128)S(1)} %copy-done.1, s32[1024]{0:T(1024)S(1)} %copy-done.5, s32[32]{0:T(128)S(1)} %copy-done.6, bf16[32,24,128]{2,1,0:T(8,128)(2,1)S(1)} %all-to-all-done.got_ref, bf16[32,128,128]{2,1,0:T(8,128)(2,1)S(1)} %copy-done.3, ...), custom_call_target="tpu_custom_call" | custom-call | flops 1073741824 | bytes 8388608 | tf_op jit(solution)/shard_map/pallas_call | solution.py:134
  29.3 12.2 %all-gather = bf16[16,4,8,512]{3,2,1,0:T(8,128)(2,1)S(1)} all-gather(bf16[4,4,8,512]{3,2,1,0:T(8,128)(2,1)S(1)} %shard_map.102), channel_id=2, replica_groups=mesh['z_lo'=4,'y'=4,'core'=2,'z_hi'=4,'x'=4] {'y'}, dimensions={0}, use_global_device_ids=true | all-gather | bytes 655360 | tf_op jit(solution)/shard_map/all_gather | solution.py:148
  41.5 4.5 %collective-permute-start = (bf16[4,4,4,8,512]{4,3,2,1,0:T(8,128)(2,1)S(1)}, bf16[4,4,4,8,512]{4,3,2,1,0:T(8,128)(2,1)S(1)}, u32[]{:S(2)}, u32[]{:S(2)}) collective-permute-start(bf16[4,4,4,8,512]{4,3,2,1,0:T(8,128)(2,1)S(1)} %bitcast.12), channel_id=1, source_target_pairs={{0,16},{16,0},{1,17},{17,1},{2,18},{18,2},{3,19},{19,3},{4,20},{20... | collective-permute-start | bytes 1572872 | tf_op jit(solution)/shard_map/ppermute | solution.py:149
  46.0 0.0 all-to-all-done.1.got_ref
  46.1 0.7 shard_map.103.w_ref
  46.7 0.8 collective-permute-done
  47.6 1.5 %shard_map.104 = bf16[4,2,128,640]{3,2,1,0:T(8,128)(2,1)S(1)} custom-call(s32[1]{0:T(128)} %bitcast.core_ref, bf16[4,128,512]{2,1,0:T(8,128)(2,1)S(1)} %bitcast.13, bf16[4,128,512]{2,1,0:T(8,128)(2,1)S(1)} %bitcast.14, bf16[512,640]{1,0:T(8,128)(2,1)S(1)} %shard_map.103.w_ref), custom_call_target="tpu_custom_call" | custom-call | tf_op jit(solution)/shard_map/pallas_call | solution.py:160
  49.1 26.7 %all_to_all.20 = bf16[32,32,640]{2,1,0:T(8,128)(2,1)S(1)} all-to-all(bf16[32,32,640]{2,1,0:T(8,128)(2,1)S(1)} %bitcast.11), channel_id=1, replica_groups=mesh['z_lo'=4,'y'=4,'core'=2,'z_hi'=4,'x'=4] {'y','core','x'}, dimensions={0} | all-to-all | bytes 2621440 | tf_op jit(solution)/shard_map/all_to_all | solution.py:175
  75.8 0.2 reduce_sum.34
  76.1 36.3 %all_to_all.21 = bf16[4,8,8,640]{3,2,1,0:T(8,128)(2,1)S(1)} all-to-all(bf16[4,8,8,640]{3,2,1,0:T(8,128)(2,1)S(1)} %copy.11), channel_id=1, replica_groups=mesh['z_lo'=4,'y'=4,'core'=2,'z_hi'=4,'x'=4] {'z_hi'}, dimensions={0} | all-to-all | bytes 655360 | tf_op jit(solution)/shard_map/all_to_all | solution.py:178
  112.4 0.7 reduce_sum.35
  (8 shorter events, 0.0 us)
Async XLA Ops:
  3.1 22.7 %copy-start.1 = (s32[32,32]{1,0:T(8,128)S(1)}, s32[32,32]{1,0:T(8,128)}, u32[]{:S(2)}) copy-start(s32[32,32]{1,0:T(8,128)} %serve_ref.1) | copy-start | bytes 12292
  3.1 22.7 %copy-start.5 = (s32[1024]{0:T(1024)S(1)}, s32[1024]{0:T(1024)}, u32[]{:S(2)}) copy-start(s32[1024]{0:T(1024)} %turn_ref.1) | copy-start | bytes 12292
  3.1 22.7 %copy-start.6 = (s32[32]{0:T(128)S(1)}, s32[32]{0:T(128)}, u32[]{:S(2)}) copy-start(s32[32]{0:T(128)} %cache_ref.1) | copy-start | bytes 388
  3.1 16.9 %all-to-all-start = ((bf16[32,24,128]{2,1,0:T(8,128)(2,1)}), bf16[32,24,128]{2,1,0:T(8,128)(2,1)S(1)}, u32[]{:S(2)}, u32[]{:S(2)}) async-start(bf16[32,24,128]{2,1,0:T(8,128)(2,1)} %shard_map.100), calls=%async_computation | async-start | bytes 393216 | tf_op jit(solution)/shard_map/all_to_all | solution.py:131
  12.2 0.9 copy-start
  13.1 12.7 %copy-start.3 = (bf16[32,128,128]{2,1,0:T(8,128)(2,1)S(1)}, bf16[32,128,128]{2,1,0:T(8,128)(2,1)}, u32[]{:S(2)}) copy-start(bf16[32,128,128]{2,1,0:T(8,128)(2,1)} %ck_ref.1) | copy-start | bytes 3145732
  20.0 26.0 %all-to-all-start.1 = ((bf16[32,80,128]{2,1,0:T(8,128)(2,1)}), bf16[32,80,128]{2,1,0:T(8,128)(2,1)S(1)}, u32[]{:S(2)}, u32[]{:S(2)}) async-start(bf16[32,80,128]{2,1,0:T(8,128)(2,1)} %shard_map.101), calls=%async_computation.1 | async-start | bytes 1310720 | tf_op jit(solution)/shard_map/all_to_all | solution.py:133
  25.9 1.2 %copy-start.4 = (bf16[32,128,128]{2,1,0:T(8,128)(2,1)S(1)}, bf16[32,128,128]{2,1,0:T(8,128)(2,1)}, u32[]{:S(2)}) copy-start(bf16[32,128,128]{2,1,0:T(8,128)(2,1)} %cv_ref.1) | copy-start | bytes 3145732
  27.1 19.0 %copy-start.2 = (s32[32]{0:T(128)S(1)}, s32[32]{0:T(128)}, u32[]{:S(2)}) copy-start(s32[32]{0:T(128)} %owner_ref.1) | copy-start | bytes 388
  41.5 6.0 %collective-permute-start = (bf16[4,4,4,8,512]{4,3,2,1,0:T(8,128)(2,1)S(1)}, bf16[4,4,4,8,512]{4,3,2,1,0:T(8,128)(2,1)S(1)}, u32[]{:S(2)}, u32[]{:S(2)}) collective-permute-start(bf16[4,4,4,8,512]{4,3,2,1,0:T(8,128)(2,1)S(1)} %bitcast.12), channel_id=1, source_target_pairs={{0,16},{16,0},{1,17},{17,1},{2,18},{18,2},{3,19},{19,3},{4,20},{20... | collective-permute-start | bytes 1572872 | tf_op jit(solution)/shard_map/ppermute | solution.py:149

commit v4 on v3

--- a/solution.py
+++ b/solution.py
@@ -20,12 +20,23 @@
 QROWS = HEADS * TURN
 VM = pl.BlockSpec(memory_space=pltpu.VMEM)
 SM = pl.BlockSpec(memory_space=pltpu.SMEM)
+HBM = pl.BlockSpec(memory_space=pltpu.HBM)
 ROOM = pltpu.CompilerParams(vmem_limit_bytes=16 << 20)
 
 
-def route_kernel(index_ref, q_ref, k_ref, v_ref, out_ref):
+def route_kernel(own_ref, serve_hbm, q_hbm, k_hbm, v_hbm, out_ref, serve_ref, q_ref, k_ref, v_ref, sems):
+    pairs = ((serve_hbm, serve_ref), (q_hbm, q_ref), (k_hbm, k_ref), (v_hbm, v_ref))
+    copies = [pltpu.make_async_copy(src, dst, sems.at[n]) for n, (src, dst) in enumerate(pairs)]
+    for copy in copies:
+        copy.start()
+    copies[0].wait()
+    serve = serve_ref[...]
+    chosen = jnp.where(serve // NREP == own_ref[0], serve % NREP, 0)
+    index = [jnp.sum(chosen[r : r + 1, :]) for r in range(NREP)]
+    for copy in copies[1:]:
+        copy.wait()
     for r in range(NREP):
-        i = index_ref[r]
+        i = index[r]
         rows = q_ref[i]
         for h in range(HEADS):
             out_ref[r, h * TURN : (h + 1) * TURN, :] = rows[:, h * HD : (h + 1) * HD]
@@ -33,17 +44,21 @@
         out_ref[r, QROWS + TURN : QROWS + 2 * TURN, :] = v_ref[i]
 
 
-def spread_kernel(w_ref, out_ref):
-    blocks = w_ref.shape[2] // NCOL // HD
-    for part in range(NCOL):
+def spread_kernel(core_ref, own_ref, other_ref, out_ref):
+    core = core_ref[0]
+    blocks = own_ref.shape[2] // NCOL // HD
+    for y in range(4):
         for j in range(blocks):
-            first = (part * blocks + j) * HD
-            piece = w_ref[0, :, first : first + HD]
-            for far in range(NREP // NCOL):
-                out_ref[far * NCOL + part, j * OWN : (j + 1) * OWN, :] = piece
-
-
-def attend_kernel(own_ref, serve_ref, turn_ref, cache_ref, got_ref, ck_ref, cv_ref, out_ref, nk, nv, s1, acc):
+            first = pl.multiple_of(core * (blocks * HD), HD) + (2 * y * blocks + j) * HD
+            for w_ref, half in ((own_ref, core), (other_ref, 1 - core)):
+                piece = w_ref[0, :, pl.ds(pl.multiple_of(first, HD), HD)]
+                for z in range(4):
+                    out_ref[z * 4 + y, half, j * OWN : (j + 1) * OWN, :] = piece
+
+
+def attend_kernel(own_ref, zhi_ref, serve_ref, turn_ref, cache_ref, got_ref, ck_ref, cv_hbm, out_ref, nk, nv, s1, acc, cv_ref, sem):
+    values = pltpu.make_async_copy(cv_hbm, cv_ref, sem)
+    values.start()
     own = own_ref[0]
     rows = SLOTS * QROWS
     scale = 1.0 / math.sqrt(HD)
@@ -70,6 +85,7 @@
     total = jnp.sum(e1 + e2, axis=1, keepdims=True)
     w1 = (e1 / total).astype(jnp.bfloat16)
     w2 = (e2 / total).astype(jnp.bfloat16)
+    values.wait()
     acc[...] = jnp.dot(w2, nv[...], preferred_element_type=jnp.float32)
     for s in range(SLOTS):
         part = slice(s * QROWS, (s + 1) * QROWS)
@@ -77,7 +93,8 @@
         live = turn_ref[serve_ref[own, s]]
         mixed = jnp.where(turn_pos < live, mixed, 0.0).astype(jnp.bfloat16)
         t = s // 2
-        z, x, at = t // 4, t % 4, (s % 2) * TURN
+        x, at = t % 4, (s % 2) * TURN
+        z = (t // 4 + 4 - zhi_ref[0]) % 4
         for h in range(HEADS):
             out_ref[x, z, at : at + TURN, h * HD : (h + 1) * HD] = mixed[h * TURN : (h + 1) * TURN, :]
 
@@ -86,7 +103,8 @@
     for b in range(NREP):
         source = owner_ref[b]
         for j in range(out_ref.shape[1] // HD):
-            out_ref[b * OWN : (b + 1) * OWN, j * HD : (j + 1) * HD] = got_ref[source, j * OWN : (j + 1) * OWN, :]
+            piece = got_ref[source // 2, source % 2, j * OWN : (j + 1) * OWN, :]
+            out_ref[b * OWN : (b + 1) * OWN, j * HD : (j + 1) * HD] = piece
 
 
 def matmul_kernel(core_ref, near_ref, far_ref, w_ref, out_ref, rows):
@@ -113,38 +131,49 @@
     own = lax.axis_index(REPL)
     out_width = new_wo.shape[2]
     width = out_width // NCOL
-    sources = serve_lists // NREP
-    send_index = jnp.sum(jnp.where(sources == own, serve_lists % NREP, 0), axis=1)
+    core = lax.axis_index("core").reshape(1)
     routed = pl.pallas_call(
         route_kernel,
         out_shape=jax.ShapeDtypeStruct((NREP, QROWS + 2 * TURN, HD), jnp.bfloat16),
-        in_specs=[SM, VM, VM, VM],
-        out_specs=VM,
-    )(send_index, queries, new_keys, new_values)
+        in_specs=[SM, HBM, HBM, HBM, HBM],
+        out_specs=VM,
+        scratch_shapes=[
+            pltpu.VMEM(serve_lists.shape, jnp.int32),
+            pltpu.VMEM(queries.shape, jnp.bfloat16),
+            pltpu.VMEM(new_keys.shape, jnp.bfloat16),
+            pltpu.VMEM(new_values.shape, jnp.bfloat16),
+            pltpu.SemaphoreType.DMA((4,)),
+        ],
+    )(own.reshape(1), serve_lists, queries, new_keys, new_values)
+    routed, shard = lax.optimization_barrier((routed, new_wo))
+    other = lax.ppermute(shard, "core", [(0, 1), (1, 0)])
     spread = pl.pallas_call(
         spread_kernel,
-        out_shape=jax.ShapeDtypeStruct((NREP, width // HD * OWN, HD), jnp.bfloat16),
-        compiler_params=ROOM,
-        in_specs=[VM],
-        out_specs=VM,
-    )(new_wo)
+        out_shape=jax.ShapeDtypeStruct((NREP // 2, 2, width // HD * OWN, HD), jnp.bfloat16),
+        compiler_params=ROOM,
+        in_specs=[SM, VM, VM],
+        out_specs=VM,
+        cost_estimate=pl.CostEstimate(flops=0, bytes_accessed=32 << 20, transcendentals=0),
+    )(core, shard, other)
     got = lax.all_to_all(routed, REPL, split_axis=0, concat_axis=0, tiled=True)
     got, spread = lax.optimization_barrier((got, spread))
-    pieces = lax.all_to_all(spread, REPL, split_axis=0, concat_axis=0, tiled=True)
+    pieces = lax.all_to_all(spread, ("z_lo", "y"), split_axis=0, concat_axis=0, tiled=True)
     attended = pl.pallas_call(
         attend_kernel,
         out_shape=jax.ShapeDtypeStruct((4, 4, 2 * TURN, HEADS * HD), jnp.bfloat16),
         compiler_params=ROOM,
-        in_specs=[SM, SM, SM, SM, VM, VM, VM],
+        in_specs=[SM, SM, SM, SM, SM, VM, VM, HBM],
         out_specs=VM,
         scratch_shapes=[
             pltpu.VMEM((SLOTS * TURN, HD), jnp.bfloat16),
             pltpu.VMEM((SLOTS * TURN, HD), jnp.bfloat16),
             pltpu.VMEM((SLOTS * QROWS, HD), jnp.float32),
             pltpu.VMEM((SLOTS * QROWS, HD), jnp.float32),
+            pltpu.VMEM(cache_values.shape, jnp.bfloat16),
+            pltpu.SemaphoreType.DMA,
         ],
         cost_estimate=pl.CostEstimate(flops=1 << 30, bytes_accessed=8 << 20, transcendentals=1 << 17),
-    )(own.reshape(1), serve_lists, turn_lens, cache_lens, got, cache_keys, cache_values)
+    )(own.reshape(1), lax.axis_index("z_hi").reshape(1), serve_lists, turn_lens, cache_lens, got, cache_keys, cache_values)
     near = lax.all_gather(attended, "y", axis=0)
     far = lax.ppermute(near, "core", [(0, 1), (1, 0)])
     weight = pl.pallas_call(
@@ -166,7 +195,7 @@
         out_specs=pl.BlockSpec((1, 2, served, width), lambda y: (y, 0, 0, 0)),
         scratch_shapes=[pltpu.VMEM((2, served, HEADS * HD), jnp.bfloat16)],
     )(
-        lax.axis_index("core").reshape(1),
+        core,
         near.reshape(4, served, HEADS * HD),
         far.reshape(4, served, HEADS * HD),
         weight,
@@ -175,8 +204,8 @@
     over_x = lax.all_to_all(partial, ("y", "core", "x"), split_axis=0, concat_axis=0, tiled=True)
     summed = jnp.sum(over_x.reshape(NCOL, 4, 4, 2 * TURN, width).astype(jnp.float32), axis=1)
     summed = jnp.transpose(summed.astype(jnp.bfloat16), (1, 0, 2, 3))
-    over_z = lax.all_to_all(summed, "z_hi", split_axis=0, concat_axis=0, tiled=True)
-    projected = jnp.sum(over_z.astype(jnp.float32), axis=0).astype(jnp.bfloat16)
+    hops = [lax.ppermute(summed[d], "z_hi", [(i, (i + d) % 4) for i in range(4)]) for d in (2, 1, 3)]
+    projected = sum(part.astype(jnp.float32) for part in [summed[0]] + hops).astype(jnp.bfloat16)
     return jnp.transpose(projected, (1, 0, 2)).reshape(1, 2 * TURN, out_width)
 
 

time: 114 us -> 108 us (0.947)
  the two profiles are of different devices: /device:TPU:65 before, /device:TPU:33 now
where the time goes in v4:
time: 108 us; the launch traced here: 107 us
  starting transfers between devices  41.1 us (38%)
  blocking collectives  40.4 us (37%)
  waiting for transfers between devices  14.6 us (14%)
  Pallas kernels  7.37 us (7%)
  local copies, waits for them, and re-layouts  2.19 us (2%)
    all_to_all x1, blocking collectives, on_device(): lax.all_to_all(partial, ('y', 'core', 'x'), split_axis=0, concat_axis=0,...  26.6 us
    ppermute x3, starting transfers between devices, on_device(): lax.ppermute(summed[d], 'z_hi', [(i, (i + d) % 4) for i in range(4)])  21.9 us
    all_gather x1, blocking collectives, on_device(): near = lax.all_gather(attended, 'y', axis=0)  13.8 us
    all_to_all x1, starting transfers between devices, on_device(): got = lax.all_to_all(routed, REPL, split_axis=0, concat_axis=0, tiled=True)  9.5 us
    ppermute x3, waiting for transfers between devices, on_device(): lax.ppermute(summed[d], 'z_hi', [(i, (i + d) % 4) for i in range(4)])  9.23 us
    all_to_all x1, starting transfers between devices, on_device(): lax.all_to_all(spread, ('z_lo', 'y'), split_axis=0, concat_axis=0, tiled=...  4.32 us
    all_to_all x1, waiting for transfers between devices, on_device(): got = lax.all_to_all(routed, REPL, split_axis=0, concat_axis=0, tiled=True)  3.51 us
    ppermute x1, starting transfers between devices, on_device(): far = lax.ppermute(near, 'core', [(0, 1), (1, 0)])  3.1 us
  transfers between devices with their start and end apart: 7, of which 5 were waited for; matrix products, arithmetic and copies ran while one was open for 0% of the time, Pallas kernels for 4%

profile of v4, /device:TPU:33, one launch (start us, length us, event | category | flops | bytes accessed | tf_op | source)
XLA Modules:
  0.0 106.8 jit_solution(1975003646179045229)
XLA Ops:
  0.0 1.7 %shard_map.100 = bf16[32,24,128]{2,1,0:T(8,128)(2,1)} custom-call(s32[1]{0:T(128)} %bitcast.1.own_ref, s32[32,32]{1,0:T(8,128)} %serve_ref.1, bf16[32,4,512]{2,1,0:T(4,128)(2,1)} %q_hbm.1, bf16[32,4,128]{2,1,0:T(4,128)(2,1)} %k_hbm.1, bf16[32,4,128]{2,1,0:T(4,128)(2,1)} %v_hbm.1), custom_call_target="tpu_custom_call" | custom-call | tf_op jit(solution)/shard_map/pallas_call | solution.py:135
  1.8 0.0 copy-start.6
  1.8 9.5 %all-to-all-start = ((bf16[32,24,128]{2,1,0:T(8,128)(2,1)}), bf16[32,24,128]{2,1,0:T(8,128)(2,1)S(1)}, u32[]{:S(2)}, u32[]{:S(2)}) async-start(bf16[32,24,128]{2,1,0:T(8,128)(2,1)} %shard_map.100), calls=%async_computation | async-start | bytes 393216 | tf_op jit(solution)/shard_map/all_to_all | solution.py:158
  11.3 2.3 %collective-permute-start = (bf16[1,16,5120]{2,1,0:T(8,128)(2,1)}, bf16[1,16,5120]{2,1,0:T(8,128)(2,1)S(1)}, u32[]{:S(2)}, u32[]{:S(2)}) collective-permute-start(bf16[1,16,5120]{2,1,0:T(8,128)(2,1)} %own_ref), channel_id=1, source_target_pairs={{0,16},{16,0},{1,17},{17,1},{2,18},{18,2},{3,19},{19,3},{4,20},{20... | collective-permute-start | bytes 491528 | tf_op jit(solution)/shard_map/ppermute | solution.py:149
  13.6 1.2 %collective-permute-done.other_ref = bf16[1,16,5120]{2,1,0:T(8,128)(2,1)S(1)} collective-permute-done((bf16[1,16,5120]{2,1,0:T(8,128)(2,1)}, bf16[1,16,5120]{2,1,0:T(8,128)(2,1)S(1)}, u32[]{:S(2)}, u32[]{:S(2)}) %collective-permute-start) | collective-permute-done | bytes 163872 | tf_op jit(solution)/shard_map/ppermute | solution.py:149
  14.8 0.9 copy-done
  15.7 0.9 shard_map.101
  16.6 3.5 %all-to-all-done.got_ref = bf16[32,24,128]{2,1,0:T(8,128)(2,1)S(1)} async-done(((bf16[32,24,128]{2,1,0:T(8,128)(2,1)}), bf16[32,24,128]{2,1,0:T(8,128)(2,1)S(1)}, u32[]{:S(2)}, u32[]{:S(2)}) %all-to-all-start) | async-done | bytes 196640 | tf_op jit(solution)/shard_map/all_to_all | solution.py:158
  20.1 4.3 %all-to-all-start.1 = ((bf16[16,2,80,128]{3,2,1,0:T(8,128)(2,1)}), bf16[16,2,80,128]{3,2,1,0:T(8,128)(2,1)S(1)}, u32[]{:S(2)}, u32[]{:S(2)}) async-start(bf16[16,2,80,128]{3,2,1,0:T(8,128)(2,1)} %shard_map.101), calls=%async_computation.1 | async-start | bytes 1310720 | tf_op jit(solution)/shard_map/all_to_all | solution.py:160
  24.5 1.2 %copy-done.4 = bf16[32,128,128]{2,1,0:T(8,128)(2,1)S(1)} copy-done((bf16[32,128,128]{2,1,0:T(8,128)(2,1)S(1)}, bf16[32,128,128]{2,1,0:T(8,128)(2,1)}, u32[]{:S(2)}) %copy-start.4) | copy-done | bytes 1048600
  25.7 2.4 %shard_map.102 = bf16[4,4,8,512]{3,2,1,0:T(8,128)(2,1)S(1)} custom-call(s32[1]{0:T(128)} %bitcast.1.own_ref, s32[1]{0:T(128)} %bitcast.2.zhi_ref, s32[32,32]{1,0:T(8,128)S(1)} %copy-done.1, s32[1024]{0:T(1024)S(1)} %copy-done.5, s32[32]{0:T(128)S(1)} %copy-done.6, bf16[32,24,128]{2,1,0:T(8,128)(2,1)S(1)} %all-to-all-done.got_ref, ...), custom_call_target="tpu_custom_call" | custom-call | flops 1073741824 | bytes 8388608 | tf_op jit(solution)/shard_map/pallas_call | solution.py:161
  28.1 13.8 %all-gather = bf16[16,4,8,512]{3,2,1,0:T(8,128)(2,1)S(1)} all-gather(bf16[4,4,8,512]{3,2,1,0:T(8,128)(2,1)S(1)} %shard_map.102), channel_id=2, replica_groups=mesh['z_lo'=4,'y'=4,'core'=2,'z_hi'=4,'x'=4] {'y'}, dimensions={0}, use_global_device_ids=true | all-gather | bytes 655360 | tf_op jit(solution)/shard_map/all_gather | solution.py:177
  41.9 3.1 %collective-permute-start.1 = (bf16[4,4,4,8,512]{4,3,2,1,0:T(8,128)(2,1)S(1)}, bf16[4,4,4,8,512]{4,3,2,1,0:T(8,128)(2,1)S(1)}, u32[]{:S(2)}, u32[]{:S(2)}) collective-permute-start(bf16[4,4,4,8,512]{4,3,2,1,0:T(8,128)(2,1)S(1)} %bitcast.30), channel_id=1, source_target_pairs={{0,16},{16,0},{1,17},{17,1},{2,18},{18,2},{3,19},{19,3},{4,20},{20... | collective-permute-start | bytes 1572872 | tf_op jit(solution)/shard_map/ppermute | solution.py:178
  45.0 0.8 shard_map.103.w_ref
  45.9 0.6 collective-permute-done.1
  46.5 1.5 %shard_map.104 = bf16[4,2,128,640]{3,2,1,0:T(8,128)(2,1)S(1)} custom-call(s32[1]{0:T(128)} %bitcast.core_ref, bf16[4,128,512]{2,1,0:T(8,128)(2,1)S(1)} %bitcast.31, bf16[4,128,512]{2,1,0:T(8,128)(2,1)S(1)} %bitcast.32, bf16[512,640]{1,0:T(8,128)(2,1)S(1)} %shard_map.103.w_ref), custom_call_target="tpu_custom_call" | custom-call | tf_op jit(solution)/shard_map/pallas_call | solution.py:189
  48.0 26.6 %all_to_all.15 = bf16[32,32,640]{2,1,0:T(8,128)(2,1)S(1)} all-to-all(bf16[32,32,640]{2,1,0:T(8,128)(2,1)S(1)} %bitcast.29), channel_id=1, replica_groups=mesh['z_lo'=4,'y'=4,'core'=2,'z_hi'=4,'x'=4] {'y','core','x'}, dimensions={0} | all-to-all | bytes 2621440 | tf_op jit(solution)/shard_map/all_to_all | solution.py:204
  74.7 0.2 reduce_sum.12
  74.9 12.7 %collective-permute-start.2 = (bf16[8,8,640]{2,1,0:T(8,128)(2,1)S(1)}, bf16[8,8,640]{2,1,0:T(8,128)(2,1)S(1)}, u32[]{:S(2)}, u32[]{:S(2)}) collective-permute-start(bf16[8,8,640]{2,1,0:T(8,128)(2,1)S(1)} %get-tuple-element.13), channel_id=1, source_target_pairs={{0,8},{4,12},{8,0},{12,4},{1,9},{5,13},{9,1},{13,5},{2,10},{6,14},... | collective-permute-start | bytes 245768 | tf_op jit(solution)/shard_map/ppermute | solution.py:207
  87.7 3.1 %collective-permute-start.4 = (bf16[8,8,640]{2,1,0:T(8,128)(2,1)S(1)}, bf16[8,8,640]{2,1,0:T(8,128)(2,1)S(1)}, u32[]{:S(2)}, u32[]{:S(2)}) collective-permute-start(bf16[8,8,640]{2,1,0:T(8,128)(2,1)S(1)} %get-tuple-element.14), channel_id=1, source_target_pairs={{0,12},{4,0},{8,4},{12,8},{1,13},{5,1},{9,5},{13,9},{2,14},{6,2},{... | collective-permute-start | bytes 245768 | tf_op jit(solution)/shard_map/ppermute | solution.py:207
  90.8 6.1 %collective-permute-start.3 = (bf16[8,8,640]{2,1,0:T(8,128)(2,1)S(1)}, bf16[8,8,640]{2,1,0:T(8,128)(2,1)S(1)}, u32[]{:S(2)}, u32[]{:S(2)}) collective-permute-start(bf16[8,8,640]{2,1,0:T(8,128)(2,1)S(1)} %get-tuple-element.15), channel_id=1, source_target_pairs={{0,4},{4,8},{8,12},{12,0},{1,5},{5,9},{9,13},{13,1},{2,6},{6,10},{... | collective-permute-start | bytes 245768 | tf_op jit(solution)/shard_map/ppermute | solution.py:207
  96.9 1.1 %collective-permute-done.4 = bf16[8,8,640]{2,1,0:T(8,128)(2,1)S(1)} collective-permute-done((bf16[8,8,640]{2,1,0:T(8,128)(2,1)S(1)}, bf16[8,8,640]{2,1,0:T(8,128)(2,1)S(1)}, u32[]{:S(2)}, u32[]{:S(2)}) %collective-permute-start.4) | collective-permute-done | bytes 81952 | tf_op jit(solution)/shard_map/ppermute | solution.py:207
  98.0 8.1 %collective-permute-done.3 = bf16[8,8,640]{2,1,0:T(8,128)(2,1)S(1)} collective-permute-done((bf16[8,8,640]{2,1,0:T(8,128)(2,1)S(1)}, bf16[8,8,640]{2,1,0:T(8,128)(2,1)S(1)}, u32[]{:S(2)}, u32[]{:S(2)}) %collective-permute-start.3) | collective-permute-done | bytes 81952 | tf_op jit(solution)/shard_map/ppermute | solution.py:207
  106.1 0.7 fusion.2
  (14 shorter events, 0.1 us)
Async XLA Ops:
  1.7 22.7 %copy-start.1 = (s32[32,32]{1,0:T(8,128)S(1)}, s32[32,32]{1,0:T(8,128)}, u32[]{:S(2)}) copy-start(s32[32,32]{1,0:T(8,128)} %serve_ref.1) | copy-start | bytes 12292
  1.8 22.7 %copy-start.5 = (s32[1024]{0:T(1024)S(1)}, s32[1024]{0:T(1024)}, u32[]{:S(2)}) copy-start(s32[1024]{0:T(1024)} %turn_ref.1) | copy-start | bytes 12292
  1.8 22.7 %copy-start.6 = (s32[32]{0:T(128)S(1)}, s32[32]{0:T(128)}, u32[]{:S(2)}) copy-start(s32[32]{0:T(128)} %cache_ref.1) | copy-start | bytes 388
  1.8 18.4 %all-to-all-start = ((bf16[32,24,128]{2,1,0:T(8,128)(2,1)}), bf16[32,24,128]{2,1,0:T(8,128)(2,1)S(1)}, u32[]{:S(2)}, u32[]{:S(2)}) async-start(bf16[32,24,128]{2,1,0:T(8,128)(2,1)} %shard_map.100), calls=%async_computation | async-start | bytes 393216 | tf_op jit(solution)/shard_map/all_to_all | solution.py:158
  11.3 3.5 %collective-permute-start = (bf16[1,16,5120]{2,1,0:T(8,128)(2,1)}, bf16[1,16,5120]{2,1,0:T(8,128)(2,1)S(1)}, u32[]{:S(2)}, u32[]{:S(2)}) collective-permute-start(bf16[1,16,5120]{2,1,0:T(8,128)(2,1)} %own_ref), channel_id=1, source_target_pairs={{0,16},{16,0},{1,17},{17,1},{2,18},{18,2},{3,19},{19,3},{4,20},{20... | collective-permute-start | bytes 491528 | tf_op jit(solution)/shard_map/ppermute | solution.py:149
  14.8 0.9 copy-start
  15.7 8.8 %copy-start.3 = (bf16[32,128,128]{2,1,0:T(8,128)(2,1)S(1)}, bf16[32,128,128]{2,1,0:T(8,128)(2,1)}, u32[]{:S(2)}) copy-start(bf16[32,128,128]{2,1,0:T(8,128)(2,1)} %ck_ref.1) | copy-start | bytes 3145732
  20.1 24.9 %all-to-all-start.1 = ((bf16[16,2,80,128]{3,2,1,0:T(8,128)(2,1)}), bf16[16,2,80,128]{3,2,1,0:T(8,128)(2,1)S(1)}, u32[]{:S(2)}, u32[]{:S(2)}) async-start(bf16[16,2,80,128]{3,2,1,0:T(8,128)(2,1)} %shard_map.101), calls=%async_computation.1 | async-start | bytes 1310720 | tf_op jit(solution)/shard_map/all_to_all | solution.py:160
  24.5 1.2 %copy-start.4 = (bf16[32,128,128]{2,1,0:T(8,128)(2,1)S(1)}, bf16[32,128,128]{2,1,0:T(8,128)(2,1)}, u32[]{:S(2)}) copy-start(bf16[32,128,128]{2,1,0:T(8,128)(2,1)} %cv_hbm.1) | copy-start | bytes 3145732
  25.7 19.3 %copy-start.2 = (s32[32]{0:T(128)S(1)}, s32[32]{0:T(128)}, u32[]{:S(2)}) copy-start(s32[32]{0:T(128)} %owner_ref.1) | copy-start | bytes 388
  41.9 4.6 %collective-permute-start.1 = (bf16[4,4,4,8,512]{4,3,2,1,0:T(8,128)(2,1)S(1)}, bf16[4,4,4,8,512]{4,3,2,1,0:T(8,128)(2,1)S(1)}, u32[]{:S(2)}, u32[]{:S(2)}) collective-permute-start(bf16[4,4,4,8,512]{4,3,2,1,0:T(8,128)(2,1)S(1)} %bitcast.30), channel_id=1, source_target_pairs={{0,16},{16,0},{1,17},{17,1},{2,18},{18,2},{3,19},{19,3},{4,20},{20... | collective-permute-start | bytes 1572872 | tf_op jit(solution)/shard_map/ppermute | solution.py:178
  74.9 22.0 %collective-permute-start.2 = (bf16[8,8,640]{2,1,0:T(8,128)(2,1)S(1)}, bf16[8,8,640]{2,1,0:T(8,128)(2,1)S(1)}, u32[]{:S(2)}, u32[]{:S(2)}) collective-permute-start(bf16[8,8,640]{2,1,0:T(8,128)(2,1)S(1)} %get-tuple-element.13), channel_id=1, source_target_pairs={{0,8},{4,12},{8,0},{12,4},{1,9},{5,13},{9,1},{13,5},{2,10},{6,14},... | collective-permute-start | bytes 245768 | tf_op jit(solution)/shard_map/ppermute | solution.py:207
  87.7 10.3 %collective-permute-start.4 = (bf16[8,8,640]{2,1,0:T(8,128)(2,1)S(1)}, bf16[8,8,640]{2,1,0:T(8,128)(2,1)S(1)}, u32[]{:S(2)}, u32[]{:S(2)}) collective-permute-start(bf16[8,8,640]{2,1,0:T(8,128)(2,1)S(1)} %get-tuple-element.14), channel_id=1, source_target_pairs={{0,12},{4,0},{8,4},{12,8},{1,13},{5,1},{9,5},{13,9},{2,14},{6,2},{... | collective-permute-start | bytes 245768 | tf_op jit(solution)/shard_map/ppermute | solution.py:207
  90.8 15.4 %collective-permute-start.3 = (bf16[8,8,640]{2,1,0:T(8,128)(2,1)S(1)}, bf16[8,8,640]{2,1,0:T(8,128)(2,1)S(1)}, u32[]{:S(2)}, u32[]{:S(2)}) collective-permute-start(bf16[8,8,640]{2,1,0:T(8,128)(2,1)S(1)} %get-tuple-element.15), channel_id=1, source_target_pairs={{0,4},{4,8},{8,12},{12,0},{1,5},{5,9},{9,13},{13,1},{2,6},{6,10},{... | collective-permute-start | bytes 245768 | tf_op jit(solution)/shard_map/ppermute | solution.py:207

commit v5 on v4

--- a/solution.py
+++ b/solution.py
@@ -15,7 +15,7 @@
 REPL = ("z_lo", "y", "core")
 TENS = ("z_hi", "x")
 NREP = 32
-NCOL = 8
+NCOL = 4
 SLOTS = 32
 QROWS = HEADS * TURN
 VM = pl.BlockSpec(memory_space=pltpu.VMEM)
@@ -44,21 +44,17 @@
         out_ref[r, QROWS + TURN : QROWS + 2 * TURN, :] = v_ref[i]
 
 
-def spread_kernel(core_ref, own_ref, other_ref, out_ref):
-    core = core_ref[0]
-    blocks = own_ref.shape[2] // NCOL // HD
-    for y in range(4):
+def spread_kernel(w_ref, out_ref):
+    blocks = w_ref.shape[2] // NCOL // HD
+    for y in range(NCOL):
         for j in range(blocks):
-            first = pl.multiple_of(core * (blocks * HD), HD) + (2 * y * blocks + j) * HD
-            for w_ref, half in ((own_ref, core), (other_ref, 1 - core)):
-                piece = w_ref[0, :, pl.ds(pl.multiple_of(first, HD), HD)]
-                for z in range(4):
-                    out_ref[z * 4 + y, half, j * OWN : (j + 1) * OWN, :] = piece
-
-
-def attend_kernel(own_ref, zhi_ref, serve_ref, turn_ref, cache_ref, got_ref, ck_ref, cv_hbm, out_ref, nk, nv, s1, acc, cv_ref, sem):
-    values = pltpu.make_async_copy(cv_hbm, cv_ref, sem)
-    values.start()
+            first = (y * blocks + j) * HD
+            piece = w_ref[0, :, first : first + HD]
+            for z in range(4):
+                out_ref[z * NCOL + y, j * OWN : (j + 1) * OWN, :] = piece
+
+
+def attend_kernel(own_ref, zhi_ref, serve_ref, turn_ref, cache_ref, got_ref, ck_ref, cv_ref, out_ref, nk, nv, s1, acc):
     own = own_ref[0]
     rows = SLOTS * QROWS
     scale = 1.0 / math.sqrt(HD)
@@ -85,7 +81,6 @@
     total = jnp.sum(e1 + e2, axis=1, keepdims=True)
     w1 = (e1 / total).astype(jnp.bfloat16)
     w2 = (e2 / total).astype(jnp.bfloat16)
-    values.wait()
     acc[...] = jnp.dot(w2, nv[...], preferred_element_type=jnp.float32)
     for s in range(SLOTS):
         part = slice(s * QROWS, (s + 1) * QROWS)
@@ -99,21 +94,19 @@
             out_ref[x, z, at : at + TURN, h * HD : (h + 1) * HD] = mixed[h * TURN : (h + 1) * TURN, :]
 
 
-def weight_kernel(owner_ref, got_ref, out_ref):
+def weight_kernel(owner_ref, core_ref, near_ref, far_ref, out_ref, both):
+    core = core_ref[0]
+    both[core] = near_ref[...]
+    both[1 - core] = far_ref[...]
     for b in range(NREP):
         source = owner_ref[b]
         for j in range(out_ref.shape[1] // HD):
-            piece = got_ref[source // 2, source % 2, j * OWN : (j + 1) * OWN, :]
+            piece = both[source % 2, source // 2, j * OWN : (j + 1) * OWN, :]
             out_ref[b * OWN : (b + 1) * OWN, j * HD : (j + 1) * HD] = piece
 
 
-def matmul_kernel(core_ref, near_ref, far_ref, w_ref, out_ref, rows):
-    core = core_ref[0]
-    rows[core] = near_ref[0]
-    rows[1 - core] = far_ref[0]
-    block = rows[...].reshape(2 * rows.shape[1], rows.shape[2])
-    product = jnp.dot(block, w_ref[...], preferred_element_type=jnp.float32).astype(jnp.bfloat16)
-    out_ref[0] = product.reshape(out_ref.shape[1:])
+def matmul_kernel(rows_ref, w_ref, out_ref):
+    out_ref[...] = jnp.dot(rows_ref[...], w_ref[...], preferred_element_type=jnp.float32).astype(jnp.bfloat16)
 
 
 def on_device(
@@ -145,16 +138,15 @@
             pltpu.SemaphoreType.DMA((4,)),
         ],
     )(own.reshape(1), serve_lists, queries, new_keys, new_values)
-    routed, shard = lax.optimization_barrier((routed, new_wo))
-    other = lax.ppermute(shard, "core", [(0, 1), (1, 0)])
+    pieces_shape = (NREP // 2, width // HD * OWN, HD)
     spread = pl.pallas_call(
         spread_kernel,
-        out_shape=jax.ShapeDtypeStruct((NREP // 2, 2, width // HD * OWN, HD), jnp.bfloat16),
-        compiler_params=ROOM,
-        in_specs=[SM, VM, VM],
-        out_specs=VM,
-        cost_estimate=pl.CostEstimate(flops=0, bytes_accessed=32 << 20, transcendentals=0),
-    )(core, shard, other)
+        out_shape=jax.ShapeDtypeStruct(pieces_shape, jnp.bfloat16),
+        compiler_params=ROOM,
+        in_specs=[VM],
+        out_specs=VM,
+        cost_estimate=pl.CostEstimate(flops=0, bytes_accessed=4 << 20, transcendentals=0),
+    )(new_wo)
     got = lax.all_to_all(routed, REPL, split_axis=0, concat_axis=0, tiled=True)
     got, spread = lax.optimization_barrier((got, spread))
     pieces = lax.all_to_all(spread, ("z_lo", "y"), split_axis=0, concat_axis=0, tiled=True)
@@ -162,46 +154,42 @@
         attend_kernel,
         out_shape=jax.ShapeDtypeStruct((4, 4, 2 * TURN, HEADS * HD), jnp.bfloat16),
         compiler_params=ROOM,
-        in_specs=[SM, SM, SM, SM, SM, VM, VM, HBM],
+        in_specs=[SM, SM, SM, SM, SM, VM, VM, VM],
         out_specs=VM,
         scratch_shapes=[
             pltpu.VMEM((SLOTS * TURN, HD), jnp.bfloat16),
             pltpu.VMEM((SLOTS * TURN, HD), jnp.bfloat16),
             pltpu.VMEM((SLOTS * QROWS, HD), jnp.float32),
             pltpu.VMEM((SLOTS * QROWS, HD), jnp.float32),
-            pltpu.VMEM(cache_values.shape, jnp.bfloat16),
-            pltpu.SemaphoreType.DMA,
         ],
         cost_estimate=pl.CostEstimate(flops=1 << 30, bytes_accessed=8 << 20, transcendentals=1 << 17),
     )(own.reshape(1), lax.axis_index("z_hi").reshape(1), serve_lists, turn_lens, cache_lens, got, cache_keys, cache_values)
-    near = lax.all_gather(attended, "y", axis=0)
-    far = lax.ppermute(near, "core", [(0, 1), (1, 0)])
+    rows = lax.all_gather(attended, "y", axis=0)
+    rows, pieces = lax.optimization_barrier((rows, pieces))
+    across = lax.ppermute(pieces, "core", [(0, 1), (1, 0)])
     weight = pl.pallas_call(
         weight_kernel,
         out_shape=jax.ShapeDtypeStruct((NREP * OWN, width), jnp.bfloat16),
         compiler_params=ROOM,
-        in_specs=[SM, VM],
-        out_specs=VM,
+        in_specs=[SM, SM, VM, VM],
+        out_specs=VM,
+        scratch_shapes=[pltpu.VMEM((2,) + pieces_shape, jnp.bfloat16)],
         cost_estimate=pl.CostEstimate(flops=0, bytes_accessed=2 * 2 * NREP * OWN * width, transcendentals=0),
-    )(owner_map, pieces)
+    )(owner_map, core, pieces, across)
     served = SLOTS * TURN
-    block = pl.BlockSpec((1, served, HEADS * HD), lambda y: (y, 0, 0))
     partial = pl.pallas_call(
         matmul_kernel,
-        out_shape=jax.ShapeDtypeStruct((4, 2, served, width), jnp.bfloat16),
-        grid=(4,),
-        compiler_params=ROOM,
-        in_specs=[SM, block, block, pl.BlockSpec((NREP * OWN, width), lambda y: (0, 0))],
-        out_specs=pl.BlockSpec((1, 2, served, width), lambda y: (y, 0, 0, 0)),
-        scratch_shapes=[pltpu.VMEM((2, served, HEADS * HD), jnp.bfloat16)],
-    )(
-        core,
-        near.reshape(4, served, HEADS * HD),
-        far.reshape(4, served, HEADS * HD),
-        weight,
-    )
-    partial = partial.reshape(NREP, NREP, width)
-    over_x = lax.all_to_all(partial, ("y", "core", "x"), split_axis=0, concat_axis=0, tiled=True)
+        out_shape=jax.ShapeDtypeStruct((NCOL * served, width), jnp.bfloat16),
+        grid=(NCOL // 2,),
+        compiler_params=ROOM,
+        in_specs=[
+            pl.BlockSpec((2 * served, HEADS * HD), lambda i: (i, 0)),
+            pl.BlockSpec((NREP * OWN, width), lambda i: (0, 0)),
+        ],
+        out_specs=pl.BlockSpec((2 * served, width), lambda i: (i, 0)),
+    )(rows.reshape(NCOL * served, HEADS * HD), weight)
+    partial = partial.reshape(NCOL * 4, 8 * TURN, width)
+    over_x = lax.all_to_all(partial, ("y", "x"), split_axis=0, concat_axis=0, tiled=True)
     summed = jnp.sum(over_x.reshape(NCOL, 4, 4, 2 * TURN, width).astype(jnp.float32), axis=1)
     summed = jnp.transpose(summed.astype(jnp.bfloat16), (1, 0, 2, 3))
     hops = [lax.ppermute(summed[d], "z_hi", [(i, (i + d) % 4) for i in range(4)]) for d in (2, 1, 3)]

time: 108 us -> 106 us (0.981)
  waiting for transfers between devices: 14.6 us -> 18.8 us
  blocking collectives: 40.4 us -> 38.6 us
  starting transfers between devices: 41.1 us -> 39.5 us
  local copies, waits for them, and re-layouts: 2.19 us -> 0.96 us
    all_to_all x1, waiting for transfers between devices: 3.51 us -> 7 us  [on_device(): got = lax.all_to_all(routed, REPL, split_axis=0, concat_axis=0, tiled=True)]
    all_to_all x1, blocking collectives: 26.6 us -> 25 us  [on_device(): lax.all_to_all(partial, ('y', 'x'), split_axis=0, concat_axis=0, tiled=True)]
    ppermute x2 -> x1, starting transfers between devices: 5.37 us -> 3.77 us  [on_device(): across = lax.ppermute(pieces, 'core', [(0, 1), (1, 0)])]
    unnamed x14, local copies, waits for them, and re-layouts: 2.16 us -> 0.94 us
  transfers between devices with their start and end apart: 7 -> 6, of which waited for: 5 -> 5; matrix products, arithmetic and copies ran while one was open for 0% -> 0% of each run, Pallas kernels for 4% -> 3%
where the time goes in v5:
time: 106 us
  starting transfers between devices  39.5 us (37%)
  blocking collectives  38.6 us (36%)
  waiting for transfers between devices  18.8 us (18%)
  Pallas kernels  6.91 us (7%)
    all_to_all x1, blocking collectives, on_device(): lax.all_to_all(partial, ('y', 'x'), split_axis=0, concat_axis=0, tiled=True)  25 us
    ppermute x3, starting transfers between devices, on_device(): lax.ppermute(summed[d], 'z_hi', [(i, (i + d) % 4) for i in range(4)])  21.9 us
    all_gather x1, blocking collectives, on_device(): rows = lax.all_gather(attended, 'y', axis=0)  13.7 us
    all_to_all x1, starting transfers between devices, on_device(): got = lax.all_to_all(routed, REPL, split_axis=0, concat_axis=0, tiled=True)  9.5 us
    ppermute x3, waiting for transfers between devices, on_device(): lax.ppermute(summed[d], 'z_hi', [(i, (i + d) % 4) for i in range(4)])  9.05 us
    all_to_all x1, waiting for transfers between devices, on_device(): got = lax.all_to_all(routed, REPL, split_axis=0, concat_axis=0, tiled=True)  7 us
    all_to_all x1, starting transfers between devices, on_device(): lax.all_to_all(spread, ('z_lo', 'y'), split_axis=0, concat_axis=0, tiled=...  4.32 us
    ppermute x1, starting transfers between devices, on_device(): across = lax.ppermute(pieces, 'core', [(0, 1), (1, 0)])  3.77 us
  transfers between devices with their start and end apart: 6, of which 5 were waited for; matrix products, arithmetic and copies ran while one was open for 0% of the time, Pallas kernels for 3%

profile of v5, /device:TPU:33, one launch (start us, length us, event | category | flops | bytes accessed | tf_op | source)
XLA Modules:
  0.0 105.9 jit_solution(5707275449635159872)
XLA Ops:
  0.0 1.7 %shard_map.100 = bf16[32,24,128]{2,1,0:T(8,128)(2,1)} custom-call(s32[1]{0:T(128)} %bitcast.own_ref, s32[32,32]{1,0:T(8,128)} %serve_ref.1, bf16[32,4,512]{2,1,0:T(4,128)(2,1)} %q_hbm.1, bf16[32,4,128]{2,1,0:T(4,128)(2,1)} %k_hbm.1, bf16[32,4,128]{2,1,0:T(4,128)(2,1)} %v_hbm.1), custom_call_target="tpu_custom_call" | custom-call | tf_op jit(solution)/shard_map/pallas_call | solution.py:128
  1.7 0.0 copy-start.5
  1.8 0.0 copy-start.6
  1.8 9.5 %all-to-all-start = ((bf16[32,24,128]{2,1,0:T(8,128)(2,1)}), bf16[32,24,128]{2,1,0:T(8,128)(2,1)S(1)}, u32[]{:S(2)}, u32[]{:S(2)}) async-start(bf16[32,24,128]{2,1,0:T(8,128)(2,1)} %shard_map.100), calls=%async_computation | async-start | bytes 393216 | tf_op jit(solution)/shard_map/all_to_all | solution.py:150
  11.3 0.0 copy-start
  11.3 0.9 copy-done
  12.2 0.9 shard_map.101
  13.1 7.0 %all-to-all-done.got_ref = bf16[32,24,128]{2,1,0:T(8,128)(2,1)S(1)} async-done(((bf16[32,24,128]{2,1,0:T(8,128)(2,1)}), bf16[32,24,128]{2,1,0:T(8,128)(2,1)S(1)}, u32[]{:S(2)}, u32[]{:S(2)}) %all-to-all-start) | async-done | bytes 196640 | tf_op jit(solution)/shard_map/all_to_all | solution.py:150
  20.1 4.3 %all-to-all-start.1 = ((bf16[16,160,128]{2,1,0:T(8,128)(2,1)}), bf16[16,160,128]{2,1,0:T(8,128)(2,1)S(1)}, u32[]{:S(2)}, u32[]{:S(2)}) async-start(bf16[16,160,128]{2,1,0:T(8,128)(2,1)} %shard_map.101), calls=%async_computation.1 | async-start | bytes 1310720 | tf_op jit(solution)/shard_map/all_to_all | solution.py:152
  24.5 2.2 %shard_map.102 = bf16[4,4,8,512]{3,2,1,0:T(8,128)(2,1)S(1)} custom-call(s32[1]{0:T(128)} %bitcast.own_ref, s32[1]{0:T(128)} %bitcast.1.zhi_ref, s32[32,32]{1,0:T(8,128)S(1)} %copy-done.1, s32[1024]{0:T(1024)S(1)} %copy-done.5, s32[32]{0:T(128)S(1)} %copy-done.6, bf16[32,24,128]{2,1,0:T(8,128)(2,1)S(1)} %all-to-all-done.got_ref, ...), custom_call_target="tpu_custom_call" | custom-call | flops 1073741824 | bytes 8388608 | tf_op jit(solution)/shard_map/pallas_call | solution.py:153
  26.7 13.7 %all-gather = bf16[16,4,8,512]{3,2,1,0:T(8,128)(2,1)S(1)} all-gather(bf16[4,4,8,512]{3,2,1,0:T(8,128)(2,1)S(1)} %shard_map.102), channel_id=2, replica_groups=mesh['z_lo'=4,'y'=4,'core'=2,'z_hi'=4,'x'=4] {'y'}, dimensions={0}, use_global_device_ids=true | all-gather | bytes 655360 | tf_op jit(solution)/shard_map/all_gather | solution.py:167
  40.4 1.0 all-to-all-done.1.near_ref
  41.4 3.8 %collective-permute-start = (bf16[16,160,128]{2,1,0:T(8,128)(2,1)S(1)}, bf16[16,160,128]{2,1,0:T(8,128)(2,1)S(1)}, u32[]{:S(2)}, u32[]{:S(2)}) collective-permute-start(bf16[16,160,128]{2,1,0:T(8,128)(2,1)S(1)} %all-to-all-done.1.near_ref), channel_id=1, source_target_pairs={{0,16},{16,0},{1,17},{17,1},{2,18},{18,2},{3,19},{19,3},{4,20},{20... | collective-permute-start | bytes 1966088 | tf_op jit(solution)/shard_map/ppermute | solution.py:169
  45.2 1.7 %collective-permute-done.far_ref = bf16[16,160,128]{2,1,0:T(8,128)(2,1)S(1)} collective-permute-done((bf16[16,160,128]{2,1,0:T(8,128)(2,1)S(1)}, bf16[16,160,128]{2,1,0:T(8,128)(2,1)S(1)}, u32[]{:S(2)}, u32[]{:S(2)}) %collective-permute-start) | collective-permute-done | bytes 655392 | tf_op jit(solution)/shard_map/ppermute | solution.py:169
  46.9 1.0 shard_map.103.w_ref
  47.9 1.0 shard_map.104
  48.9 25.0 %all_to_all.15 = bf16[16,32,1280]{2,1,0:T(8,128)(2,1)S(1)} all-to-all(bf16[16,32,1280]{2,1,0:T(8,128)(2,1)S(1)} %bitcast.28), channel_id=1, replica_groups=mesh['z_lo'=4,'y'=4,'core'=2,'z_hi'=4,'x'=4] {'y','x'}, dimensions={0} | all-to-all | bytes 2621440 | tf_op jit(solution)/shard_map/all_to_all | solution.py:192
  73.9 0.2 reduce_sum.12
  74.2 12.7 %collective-permute-start.1 = (bf16[4,8,1280]{2,1,0:T(8,128)(2,1)S(1)}, bf16[4,8,1280]{2,1,0:T(8,128)(2,1)S(1)}, u32[]{:S(2)}, u32[]{:S(2)}) collective-permute-start(bf16[4,8,1280]{2,1,0:T(8,128)(2,1)S(1)} %get-tuple-element.13), channel_id=1, source_target_pairs={{0,8},{4,12},{8,0},{12,4},{1,9},{5,13},{9,1},{13,5},{2,10},{6,14},... | collective-permute-start | bytes 245768 | tf_op jit(solution)/shard_map/ppermute | solution.py:195
  86.9 3.1 %collective-permute-start.3 = (bf16[4,8,1280]{2,1,0:T(8,128)(2,1)S(1)}, bf16[4,8,1280]{2,1,0:T(8,128)(2,1)S(1)}, u32[]{:S(2)}, u32[]{:S(2)}) collective-permute-start(bf16[4,8,1280]{2,1,0:T(8,128)(2,1)S(1)} %get-tuple-element.14), channel_id=1, source_target_pairs={{0,12},{4,0},{8,4},{12,8},{1,13},{5,1},{9,5},{13,9},{2,14},{6,2},{... | collective-permute-start | bytes 245768 | tf_op jit(solution)/shard_map/ppermute | solution.py:195
  90.0 6.1 %collective-permute-start.2 = (bf16[4,8,1280]{2,1,0:T(8,128)(2,1)S(1)}, bf16[4,8,1280]{2,1,0:T(8,128)(2,1)S(1)}, u32[]{:S(2)}, u32[]{:S(2)}) collective-permute-start(bf16[4,8,1280]{2,1,0:T(8,128)(2,1)S(1)} %get-tuple-element.15), channel_id=1, source_target_pairs={{0,4},{4,8},{8,12},{12,0},{1,5},{5,9},{9,13},{13,1},{2,6},{6,10},{... | collective-permute-start | bytes 245768 | tf_op jit(solution)/shard_map/ppermute | solution.py:195
  96.1 2.4 %collective-permute-done.3 = bf16[4,8,1280]{2,1,0:T(8,128)(2,1)S(1)} collective-permute-done((bf16[4,8,1280]{2,1,0:T(8,128)(2,1)S(1)}, bf16[4,8,1280]{2,1,0:T(8,128)(2,1)S(1)}, u32[]{:S(2)}, u32[]{:S(2)}) %collective-permute-start.3) | collective-permute-done | bytes 81952 | tf_op jit(solution)/shard_map/ppermute | solution.py:195
  98.5 6.7 %collective-permute-done.2 = bf16[4,8,1280]{2,1,0:T(8,128)(2,1)S(1)} collective-permute-done((bf16[4,8,1280]{2,1,0:T(8,128)(2,1)S(1)}, bf16[4,8,1280]{2,1,0:T(8,128)(2,1)S(1)}, u32[]{:S(2)}, u32[]{:S(2)}) %collective-permute-start.2) | collective-permute-done | bytes 81952 | tf_op jit(solution)/shard_map/ppermute | solution.py:195
  105.2 0.7 fusion.2
  (12 shorter events, 0.0 us)
Async XLA Ops:
  1.7 22.7 %copy-start.1 = (s32[32,32]{1,0:T(8,128)S(1)}, s32[32,32]{1,0:T(8,128)}, u32[]{:S(2)}) copy-start(s32[32,32]{1,0:T(8,128)} %serve_ref.1) | copy-start | bytes 12292
  1.7 22.7 %copy-start.5 = (s32[1024]{0:T(1024)S(1)}, s32[1024]{0:T(1024)}, u32[]{:S(2)}) copy-start(s32[1024]{0:T(1024)} %turn_ref.1) | copy-start | bytes 12292
  1.8 22.7 %copy-start.6 = (s32[32]{0:T(128)S(1)}, s32[32]{0:T(128)}, u32[]{:S(2)}) copy-start(s32[32]{0:T(128)} %cache_ref.1) | copy-start | bytes 388
  1.8 18.4 %all-to-all-start = ((bf16[32,24,128]{2,1,0:T(8,128)(2,1)}), bf16[32,24,128]{2,1,0:T(8,128)(2,1)S(1)}, u32[]{:S(2)}, u32[]{:S(2)}) async-start(bf16[32,24,128]{2,1,0:T(8,128)(2,1)} %shard_map.100), calls=%async_computation | async-start | bytes 393216 | tf_op jit(solution)/shard_map/all_to_all | solution.py:150
  11.3 0.9 copy-start
  12.2 12.3 %copy-start.3 = (bf16[32,128,128]{2,1,0:T(8,128)(2,1)S(1)}, bf16[32,128,128]{2,1,0:T(8,128)(2,1)}, u32[]{:S(2)}) copy-start(bf16[32,128,128]{2,1,0:T(8,128)(2,1)} %ck_ref.1) | copy-start | bytes 3145732
  12.2 12.3 %copy-start.4 = (bf16[32,128,128]{2,1,0:T(8,128)(2,1)S(1)}, bf16[32,128,128]{2,1,0:T(8,128)(2,1)}, u32[]{:S(2)}) copy-start(bf16[32,128,128]{2,1,0:T(8,128)(2,1)} %cv_ref.1) | copy-start | bytes 3145732
  20.1 21.3 %all-to-all-start.1 = ((bf16[16,160,128]{2,1,0:T(8,128)(2,1)}), bf16[16,160,128]{2,1,0:T(8,128)(2,1)S(1)}, u32[]{:S(2)}, u32[]{:S(2)}) async-start(bf16[16,160,128]{2,1,0:T(8,128)(2,1)} %shard_map.101), calls=%async_computation.1 | async-start | bytes 1310720 | tf_op jit(solution)/shard_map/all_to_all | solution.py:152
  24.5 22.4 %copy-start.2 = (s32[32]{0:T(128)S(1)}, s32[32]{0:T(128)}, u32[]{:S(2)}) copy-start(s32[32]{0:T(128)} %owner_ref.1) | copy-start | bytes 388
  41.4 5.5 %collective-permute-start = (bf16[16,160,128]{2,1,0:T(8,128)(2,1)S(1)}, bf16[16,160,128]{2,1,0:T(8,128)(2,1)S(1)}, u32[]{:S(2)}, u32[]{:S(2)}) collective-permute-start(bf16[16,160,128]{2,1,0:T(8,128)(2,1)S(1)} %all-to-all-done.1.near_ref), channel_id=1, source_target_pairs={{0,16},{16,0},{1,17},{17,1},{2,18},{18,2},{3,19},{19,3},{4,20},{20... | collective-permute-start | bytes 1966088 | tf_op jit(solution)/shard_map/ppermute | solution.py:169
  74.2 22.0 %collective-permute-start.1 = (bf16[4,8,1280]{2,1,0:T(8,128)(2,1)S(1)}, bf16[4,8,1280]{2,1,0:T(8,128)(2,1)S(1)}, u32[]{:S(2)}, u32[]{:S(2)}) collective-permute-start(bf16[4,8,1280]{2,1,0:T(8,128)(2,1)S(1)} %get-tuple-element.13), channel_id=1, source_target_pairs={{0,8},{4,12},{8,0},{12,4},{1,9},{5,13},{9,1},{13,5},{2,10},{6,14},... | collective-permute-start | bytes 245768 | tf_op jit(solution)/shard_map/ppermute | solution.py:195
  86.9 11.6 %collective-permute-start.3 = (bf16[4,8,1280]{2,1,0:T(8,128)(2,1)S(1)}, bf16[4,8,1280]{2,1,0:T(8,128)(2,1)S(1)}, u32[]{:S(2)}, u32[]{:S(2)}) collective-permute-start(bf16[4,8,1280]{2,1,0:T(8,128)(2,1)S(1)} %get-tuple-element.14), channel_id=1, source_target_pairs={{0,12},{4,0},{8,4},{12,8},{1,13},{5,1},{9,5},{13,9},{2,14},{6,2},{... | collective-permute-start | bytes 245768 | tf_op jit(solution)/shard_map/ppermute | solution.py:195
  90.0 15.2 %collective-permute-start.2 = (bf16[4,8,1280]{2,1,0:T(8,128)(2,1)S(1)}, bf16[4,8,1280]{2,1,0:T(8,128)(2,1)S(1)}, u32[]{:S(2)}, u32[]{:S(2)}) collective-permute-start(bf16[4,8,1280]{2,1,0:T(8,128)(2,1)S(1)} %get-tuple-element.15), channel_id=1, source_target_pairs={{0,4},{4,8},{8,12},{12,0},{1,5},{5,9},{9,13},{13,1},{2,6},{6,10},{... | collective-permute-start | bytes 245768 | tf_op jit(solution)/shard_map/ppermute | solution.py:195

commit v6 on v5

--- a/solution.py
+++ b/solution.py
@@ -106,7 +106,11 @@
 
 
 def matmul_kernel(rows_ref, w_ref, out_ref):
-    out_ref[...] = jnp.dot(rows_ref[...], w_ref[...], preferred_element_type=jnp.float32).astype(jnp.bfloat16)
+    product = jnp.dot(rows_ref[...], w_ref[...], preferred_element_type=jnp.float32).astype(jnp.bfloat16)
+    for y in range(out_ref.shape[1]):
+        for x in range(out_ref.shape[0]):
+            first = (y * out_ref.shape[0] + x) * out_ref.shape[2]
+            out_ref[x, y] = product[first : first + out_ref.shape[2], :]
 
 
 def on_device(
@@ -179,18 +183,18 @@
     served = SLOTS * TURN
     partial = pl.pallas_call(
         matmul_kernel,
-        out_shape=jax.ShapeDtypeStruct((NCOL * served, width), jnp.bfloat16),
+        out_shape=jax.ShapeDtypeStruct((4, NCOL, 8 * TURN, width), jnp.bfloat16),
         grid=(NCOL // 2,),
         compiler_params=ROOM,
         in_specs=[
             pl.BlockSpec((2 * served, HEADS * HD), lambda i: (i, 0)),
             pl.BlockSpec((NREP * OWN, width), lambda i: (0, 0)),
         ],
-        out_specs=pl.BlockSpec((2 * served, width), lambda i: (i, 0)),
+        out_specs=pl.BlockSpec((4, 2, 8 * TURN, width), lambda i: (0, i, 0, 0)),
     )(rows.reshape(NCOL * served, HEADS * HD), weight)
     partial = partial.reshape(NCOL * 4, 8 * TURN, width)
-    over_x = lax.all_to_all(partial, ("y", "x"), split_axis=0, concat_axis=0, tiled=True)
-    summed = jnp.sum(over_x.reshape(NCOL, 4, 4, 2 * TURN, width).astype(jnp.float32), axis=1)
+    over_x = lax.all_to_all(partial, ("x", "y"), split_axis=0, concat_axis=0, tiled=True)
+    summed = jnp.sum(over_x.reshape(4, NCOL, 4, 2 * TURN, width).astype(jnp.float32), axis=0)
     summed = jnp.transpose(summed.astype(jnp.bfloat16), (1, 0, 2, 3))
     hops = [lax.ppermute(summed[d], "z_hi", [(i, (i + d) % 4) for i in range(4)]) for d in (2, 1, 3)]
     projected = sum(part.astype(jnp.float32) for part in [summed[0]] + hops).astype(jnp.bfloat16)

time: 106 us -> 106 us (level)
  no operation moved by 1% of the time
where the time goes in v6:
time: 106 us; the launch traced here: 105 us
  starting transfers between devices  39.5 us (37%)
  blocking collectives  38.1 us (36%)
  waiting for transfers between devices  18.7 us (18%)
  Pallas kernels  6.98 us (7%)
    all_to_all x1, blocking collectives, on_device(): lax.all_to_all(partial, ('x', 'y'), split_axis=0, concat_axis=0, tiled=True)  24.4 us
    ppermute x3, starting transfers between devices, on_device(): lax.ppermute(summed[d], 'z_hi', [(i, (i + d) % 4) for i in range(4)])  21.9 us
    all_gather x1, blocking collectives, on_device(): rows = lax.all_gather(attended, 'y', axis=0)  13.7 us
    all_to_all x1, starting transfers between devices, on_device(): got = lax.all_to_all(routed, REPL, split_axis=0, concat_axis=0, tiled=True)  9.5 us
    ppermute x3, waiting for transfers between devices, on_device(): lax.ppermute(summed[d], 'z_hi', [(i, (i + d) % 4) for i in range(4)])  9.01 us
    all_to_all x1, waiting for transfers between devices, on_device(): got = lax.all_to_all(routed, REPL, split_axis=0, concat_axis=0, tiled=True)  7 us
    all_to_all x1, starting transfers between devices, on_device(): lax.all_to_all(spread, ('z_lo', 'y'), split_axis=0, concat_axis=0, tiled=...  4.32 us
    ppermute x1, starting transfers between devices, on_device(): across = lax.ppermute(pieces, 'core', [(0, 1), (1, 0)])  3.77 us
  transfers between devices with their start and end apart: 6, of which 5 were waited for; matrix products, arithmetic and copies ran while one was open for 0% of the time, Pallas kernels for 3%

profile of v6, /device:TPU:33, one launch (start us, length us, event | category | flops | bytes accessed | tf_op | source)
XLA Modules:
  0.0 105.4 jit_solution(6566983618828823184)
XLA Ops:
  0.0 1.7 %shard_map.100 = bf16[32,24,128]{2,1,0:T(8,128)(2,1)} custom-call(s32[1]{0:T(128)} %bitcast.own_ref, s32[32,32]{1,0:T(8,128)} %serve_ref.1, bf16[32,4,512]{2,1,0:T(4,128)(2,1)} %q_hbm.1, bf16[32,4,128]{2,1,0:T(4,128)(2,1)} %k_hbm.1, bf16[32,4,128]{2,1,0:T(4,128)(2,1)} %v_hbm.1), custom_call_target="tpu_custom_call" | custom-call | tf_op jit(solution)/shard_map/pallas_call | solution.py:132
  1.7 0.0 copy-start.5
  1.8 0.0 copy-start.6
  1.8 9.5 %all-to-all-start = ((bf16[32,24,128]{2,1,0:T(8,128)(2,1)}), bf16[32,24,128]{2,1,0:T(8,128)(2,1)S(1)}, u32[]{:S(2)}, u32[]{:S(2)}) async-start(bf16[32,24,128]{2,1,0:T(8,128)(2,1)} %shard_map.100), calls=%async_computation | async-start | bytes 393216 | tf_op jit(solution)/shard_map/all_to_all | solution.py:154
  11.3 0.0 copy-start
  11.3 0.9 copy-done
  12.2 0.9 shard_map.101
  13.1 7.0 %all-to-all-done.got_ref = bf16[32,24,128]{2,1,0:T(8,128)(2,1)S(1)} async-done(((bf16[32,24,128]{2,1,0:T(8,128)(2,1)}), bf16[32,24,128]{2,1,0:T(8,128)(2,1)S(1)}, u32[]{:S(2)}, u32[]{:S(2)}) %all-to-all-start) | async-done | bytes 196640 | tf_op jit(solution)/shard_map/all_to_all | solution.py:154
  20.1 4.3 %all-to-all-start.1 = ((bf16[16,160,128]{2,1,0:T(8,128)(2,1)}), bf16[16,160,128]{2,1,0:T(8,128)(2,1)S(1)}, u32[]{:S(2)}, u32[]{:S(2)}) async-start(bf16[16,160,128]{2,1,0:T(8,128)(2,1)} %shard_map.101), calls=%async_computation.1 | async-start | bytes 1310720 | tf_op jit(solution)/shard_map/all_to_all | solution.py:156
  24.5 2.2 %shard_map.102 = bf16[4,4,8,512]{3,2,1,0:T(8,128)(2,1)S(1)} custom-call(s32[1]{0:T(128)} %bitcast.own_ref, s32[1]{0:T(128)} %bitcast.1.zhi_ref, s32[32,32]{1,0:T(8,128)S(1)} %copy-done.1, s32[1024]{0:T(1024)S(1)} %copy-done.5, s32[32]{0:T(128)S(1)} %copy-done.6, bf16[32,24,128]{2,1,0:T(8,128)(2,1)S(1)} %all-to-all-done.got_ref, ...), custom_call_target="tpu_custom_call" | custom-call | flops 1073741824 | bytes 8388608 | tf_op jit(solution)/shard_map/pallas_call | solution.py:157
  26.7 13.7 %all-gather = bf16[16,4,8,512]{3,2,1,0:T(8,128)(2,1)S(1)} all-gather(bf16[4,4,8,512]{3,2,1,0:T(8,128)(2,1)S(1)} %shard_map.102), channel_id=2, replica_groups=mesh['z_lo'=4,'y'=4,'core'=2,'z_hi'=4,'x'=4] {'y'}, dimensions={0}, use_global_device_ids=true | all-gather | bytes 655360 | tf_op jit(solution)/shard_map/all_gather | solution.py:171
  40.4 1.0 all-to-all-done.1.near_ref
  41.4 3.8 %collective-permute-start = (bf16[16,160,128]{2,1,0:T(8,128)(2,1)S(1)}, bf16[16,160,128]{2,1,0:T(8,128)(2,1)S(1)}, u32[]{:S(2)}, u32[]{:S(2)}) collective-permute-start(bf16[16,160,128]{2,1,0:T(8,128)(2,1)S(1)} %all-to-all-done.1.near_ref), channel_id=1, source_target_pairs={{0,16},{16,0},{1,17},{17,1},{2,18},{18,2},{3,19},{19,3},{4,20},{20... | collective-permute-start | bytes 1966088 | tf_op jit(solution)/shard_map/ppermute | solution.py:173
  45.2 1.7 %collective-permute-done.far_ref = bf16[16,160,128]{2,1,0:T(8,128)(2,1)S(1)} collective-permute-done((bf16[16,160,128]{2,1,0:T(8,128)(2,1)S(1)}, bf16[16,160,128]{2,1,0:T(8,128)(2,1)S(1)}, u32[]{:S(2)}, u32[]{:S(2)}) %collective-permute-start) | collective-permute-done | bytes 655392 | tf_op jit(solution)/shard_map/ppermute | solution.py:173
  46.9 1.0 shard_map.103.w_ref
  47.9 1.1 %shard_map.104 = bf16[4,4,32,1280]{3,2,1,0:T(8,128)(2,1)S(1)} custom-call(bf16[512,512]{1,0:T(8,128)(2,1)S(1)} %bitcast.29, bf16[512,1280]{1,0:T(8,128)(2,1)S(1)} %shard_map.103.w_ref), custom_call_target="tpu_custom_call" | custom-call | tf_op jit(solution)/shard_map/pallas_call | solution.py:184
  49.0 24.4 %all_to_all.15 = bf16[16,32,1280]{2,1,0:T(8,128)(2,1)S(1)} all-to-all(bf16[16,32,1280]{2,1,0:T(8,128)(2,1)S(1)} %bitcast.28), channel_id=1, replica_groups=mesh['z_lo'=4,'y'=4,'core'=2,'z_hi'=4,'x'=4] {'x','y'}, dimensions={0} | all-to-all | bytes 2621440 | tf_op jit(solution)/shard_map/all_to_all | solution.py:196
  73.5 0.2 reduce_sum.12
  73.7 12.7 %collective-permute-start.1 = (bf16[4,8,1280]{2,1,0:T(8,128)(2,1)S(1)}, bf16[4,8,1280]{2,1,0:T(8,128)(2,1)S(1)}, u32[]{:S(2)}, u32[]{:S(2)}) collective-permute-start(bf16[4,8,1280]{2,1,0:T(8,128)(2,1)S(1)} %get-tuple-element.13), channel_id=1, source_target_pairs={{0,8},{4,12},{8,0},{12,4},{1,9},{5,13},{9,1},{13,5},{2,10},{6,14},... | collective-permute-start | bytes 245768 | tf_op jit(solution)/shard_map/ppermute | solution.py:199
  86.4 3.1 %collective-permute-start.3 = (bf16[4,8,1280]{2,1,0:T(8,128)(2,1)S(1)}, bf16[4,8,1280]{2,1,0:T(8,128)(2,1)S(1)}, u32[]{:S(2)}, u32[]{:S(2)}) collective-permute-start(bf16[4,8,1280]{2,1,0:T(8,128)(2,1)S(1)} %get-tuple-element.14), channel_id=1, source_target_pairs={{0,12},{4,0},{8,4},{12,8},{1,13},{5,1},{9,5},{13,9},{2,14},{6,2},{... | collective-permute-start | bytes 245768 | tf_op jit(solution)/shard_map/ppermute | solution.py:199
  89.5 6.1 %collective-permute-start.2 = (bf16[4,8,1280]{2,1,0:T(8,128)(2,1)S(1)}, bf16[4,8,1280]{2,1,0:T(8,128)(2,1)S(1)}, u32[]{:S(2)}, u32[]{:S(2)}) collective-permute-start(bf16[4,8,1280]{2,1,0:T(8,128)(2,1)S(1)} %get-tuple-element.15), channel_id=1, source_target_pairs={{0,4},{4,8},{8,12},{12,0},{1,5},{5,9},{9,13},{13,1},{2,6},{6,10},{... | collective-permute-start | bytes 245768 | tf_op jit(solution)/shard_map/ppermute | solution.py:199
  95.7 2.5 %collective-permute-done.3 = bf16[4,8,1280]{2,1,0:T(8,128)(2,1)S(1)} collective-permute-done((bf16[4,8,1280]{2,1,0:T(8,128)(2,1)S(1)}, bf16[4,8,1280]{2,1,0:T(8,128)(2,1)S(1)}, u32[]{:S(2)}, u32[]{:S(2)}) %collective-permute-start.3) | collective-permute-done | bytes 81952 | tf_op jit(solution)/shard_map/ppermute | solution.py:199
  98.1 6.6 %collective-permute-done.2 = bf16[4,8,1280]{2,1,0:T(8,128)(2,1)S(1)} collective-permute-done((bf16[4,8,1280]{2,1,0:T(8,128)(2,1)S(1)}, bf16[4,8,1280]{2,1,0:T(8,128)(2,1)S(1)}, u32[]{:S(2)}, u32[]{:S(2)}) %collective-permute-start.2) | collective-permute-done | bytes 81952 | tf_op jit(solution)/shard_map/ppermute | solution.py:199
  104.7 0.7 fusion.2
  (12 shorter events, 0.0 us)
Async XLA Ops:
  1.7 22.7 %copy-start.1 = (s32[32,32]{1,0:T(8,128)S(1)}, s32[32,32]{1,0:T(8,128)}, u32[]{:S(2)}) copy-start(s32[32,32]{1,0:T(8,128)} %serve_ref.1) | copy-start | bytes 12292
  1.7 22.7 %copy-start.5 = (s32[1024]{0:T(1024)S(1)}, s32[1024]{0:T(1024)}, u32[]{:S(2)}) copy-start(s32[1024]{0:T(1024)} %turn_ref.1) | copy-start | bytes 12292
  1.8 22.7 %copy-start.6 = (s32[32]{0:T(128)S(1)}, s32[32]{0:T(128)}, u32[]{:S(2)}) copy-start(s32[32]{0:T(128)} %cache_ref.1) | copy-start | bytes 388
  1.8 18.4 %all-to-all-start = ((bf16[32,24,128]{2,1,0:T(8,128)(2,1)}), bf16[32,24,128]{2,1,0:T(8,128)(2,1)S(1)}, u32[]{:S(2)}, u32[]{:S(2)}) async-start(bf16[32,24,128]{2,1,0:T(8,128)(2,1)} %shard_map.100), calls=%async_computation | async-start | bytes 393216 | tf_op jit(solution)/shard_map/all_to_all | solution.py:154
  11.3 0.9 copy-start
  12.2 12.3 %copy-start.3 = (bf16[32,128,128]{2,1,0:T(8,128)(2,1)S(1)}, bf16[32,128,128]{2,1,0:T(8,128)(2,1)}, u32[]{:S(2)}) copy-start(bf16[32,128,128]{2,1,0:T(8,128)(2,1)} %ck_ref.1) | copy-start | bytes 3145732
  12.2 12.3 %copy-start.4 = (bf16[32,128,128]{2,1,0:T(8,128)(2,1)S(1)}, bf16[32,128,128]{2,1,0:T(8,128)(2,1)}, u32[]{:S(2)}) copy-start(bf16[32,128,128]{2,1,0:T(8,128)(2,1)} %cv_ref.1) | copy-start | bytes 3145732
  20.1 21.3 %all-to-all-start.1 = ((bf16[16,160,128]{2,1,0:T(8,128)(2,1)}), bf16[16,160,128]{2,1,0:T(8,128)(2,1)S(1)}, u32[]{:S(2)}, u32[]{:S(2)}) async-start(bf16[16,160,128]{2,1,0:T(8,128)(2,1)} %shard_map.101), calls=%async_computation.1 | async-start | bytes 1310720 | tf_op jit(solution)/shard_map/all_to_all | solution.py:156
  24.5 22.4 %copy-start.2 = (s32[32]{0:T(128)S(1)}, s32[32]{0:T(128)}, u32[]{:S(2)}) copy-start(s32[32]{0:T(128)} %owner_ref.1) | copy-start | bytes 388
  41.4 5.5 %collective-permute-start = (bf16[16,160,128]{2,1,0:T(8,128)(2,1)S(1)}, bf16[16,160,128]{2,1,0:T(8,128)(2,1)S(1)}, u32[]{:S(2)}, u32[]{:S(2)}) collective-permute-start(bf16[16,160,128]{2,1,0:T(8,128)(2,1)S(1)} %all-to-all-done.1.near_ref), channel_id=1, source_target_pairs={{0,16},{16,0},{1,17},{17,1},{2,18},{18,2},{3,19},{19,3},{4,20},{20... | collective-permute-start | bytes 1966088 | tf_op jit(solution)/shard_map/ppermute | solution.py:173
  73.7 22.0 %collective-permute-start.1 = (bf16[4,8,1280]{2,1,0:T(8,128)(2,1)S(1)}, bf16[4,8,1280]{2,1,0:T(8,128)(2,1)S(1)}, u32[]{:S(2)}, u32[]{:S(2)}) collective-permute-start(bf16[4,8,1280]{2,1,0:T(8,128)(2,1)S(1)} %get-tuple-element.13), channel_id=1, source_target_pairs={{0,8},{4,12},{8,0},{12,4},{1,9},{5,13},{9,1},{13,5},{2,10},{6,14},... | collective-permute-start | bytes 245768 | tf_op jit(solution)/shard_map/ppermute | solution.py:199
  86.4 11.7 %collective-permute-start.3 = (bf16[4,8,1280]{2,1,0:T(8,128)(2,1)S(1)}, bf16[4,8,1280]{2,1,0:T(8,128)(2,1)S(1)}, u32[]{:S(2)}, u32[]{:S(2)}) collective-permute-start(bf16[4,8,1280]{2,1,0:T(8,128)(2,1)S(1)} %get-tuple-element.14), channel_id=1, source_target_pairs={{0,12},{4,0},{8,4},{12,8},{1,13},{5,1},{9,5},{13,9},{2,14},{6,2},{... | collective-permute-start | bytes 245768 | tf_op jit(solution)/shard_map/ppermute | solution.py:199
  89.5 15.1 %collective-permute-start.2 = (bf16[4,8,1280]{2,1,0:T(8,128)(2,1)S(1)}, bf16[4,8,1280]{2,1,0:T(8,128)(2,1)S(1)}, u32[]{:S(2)}, u32[]{:S(2)}) collective-permute-start(bf16[4,8,1280]{2,1,0:T(8,128)(2,1)S(1)} %get-tuple-element.15), channel_id=1, source_target_pairs={{0,4},{4,8},{8,12},{12,0},{1,5},{5,9},{9,13},{13,1},{2,6},{6,10},{... | collective-permute-start | bytes 245768 | tf_op jit(solution)/shard_map/ppermute | solution.py:199

commit v7 on v6

--- a/solution.py
+++ b/solution.py
@@ -184,13 +184,9 @@
     partial = pl.pallas_call(
         matmul_kernel,
         out_shape=jax.ShapeDtypeStruct((4, NCOL, 8 * TURN, width), jnp.bfloat16),
-        grid=(NCOL // 2,),
-        compiler_params=ROOM,
-        in_specs=[
-            pl.BlockSpec((2 * served, HEADS * HD), lambda i: (i, 0)),
-            pl.BlockSpec((NREP * OWN, width), lambda i: (0, 0)),
-        ],
-        out_specs=pl.BlockSpec((4, 2, 8 * TURN, width), lambda i: (0, i, 0, 0)),
+        compiler_params=ROOM,
+        in_specs=[VM, VM],
+        out_specs=VM,
     )(rows.reshape(NCOL * served, HEADS * HD), weight)
     partial = partial.reshape(NCOL * 4, 8 * TURN, width)
     over_x = lax.all_to_all(partial, ("x", "y"), split_axis=0, concat_axis=0, tiled=True)

time: 106 us -> 106 us (level)
  no operation moved by 1% of the time
where the time goes in v7:
time: 106 us; the launch traced here: 105 us
  starting transfers between devices  39.5 us (37%)
  blocking collectives  38.1 us (36%)
  waiting for transfers between devices  18.7 us (18%)
  Pallas kernels  6.71 us (6%)
    all_to_all x1, blocking collectives, on_device(): lax.all_to_all(partial, ('x', 'y'), split_axis=0, concat_axis=0, tiled=True)  24.4 us
    ppermute x3, starting transfers between devices, on_device(): lax.ppermute(summed[d], 'z_hi', [(i, (i + d) % 4) for i in range(4)])  21.9 us
    all_gather x1, blocking collectives, on_device(): rows = lax.all_gather(attended, 'y', axis=0)  13.7 us
    all_to_all x1, starting transfers between devices, on_device(): got = lax.all_to_all(routed, REPL, split_axis=0, concat_axis=0, tiled=True)  9.5 us
    ppermute x3, waiting for transfers between devices, on_device(): lax.ppermute(summed[d], 'z_hi', [(i, (i + d) % 4) for i in range(4)])  9.01 us
    all_to_all x1, waiting for transfers between devices, on_device(): got = lax.all_to_all(routed, REPL, split_axis=0, concat_axis=0, tiled=True)  7 us
    all_to_all x1, starting transfers between devices, on_device(): lax.all_to_all(spread, ('z_lo', 'y'), split_axis=0, concat_axis=0, tiled=...  4.32 us
    ppermute x1, starting transfers between devices, on_device(): across = lax.ppermute(pieces, 'core', [(0, 1), (1, 0)])  3.77 us
  transfers between devices with their start and end apart: 6, of which 5 were waited for; matrix products, arithmetic and copies ran while one was open for 0% of the time, Pallas kernels for 3%

profile of v7, /device:TPU:33, one launch (start us, length us, event | category | flops | bytes accessed | tf_op | source)
XLA Modules:
  0.0 105.1 jit_solution(13269316300093204165)
XLA Ops:
  0.0 1.7 %shard_map.100 = bf16[32,24,128]{2,1,0:T(8,128)(2,1)} custom-call(s32[1]{0:T(128)} %bitcast.own_ref, s32[32,32]{1,0:T(8,128)} %serve_ref.1, bf16[32,4,512]{2,1,0:T(4,128)(2,1)} %q_hbm.1, bf16[32,4,128]{2,1,0:T(4,128)(2,1)} %k_hbm.1, bf16[32,4,128]{2,1,0:T(4,128)(2,1)} %v_hbm.1), custom_call_target="tpu_custom_call" | custom-call | tf_op jit(solution)/shard_map/pallas_call | solution.py:132
  1.7 0.0 copy-start.5
  1.8 0.0 copy-start.6
  1.8 9.5 %all-to-all-start = ((bf16[32,24,128]{2,1,0:T(8,128)(2,1)}), bf16[32,24,128]{2,1,0:T(8,128)(2,1)S(1)}, u32[]{:S(2)}, u32[]{:S(2)}) async-start(bf16[32,24,128]{2,1,0:T(8,128)(2,1)} %shard_map.100), calls=%async_computation | async-start | bytes 393216 | tf_op jit(solution)/shard_map/all_to_all | solution.py:154
  11.3 0.0 copy-start
  11.3 0.9 copy-done
  12.2 0.9 shard_map.101
  13.1 7.0 %all-to-all-done.got_ref = bf16[32,24,128]{2,1,0:T(8,128)(2,1)S(1)} async-done(((bf16[32,24,128]{2,1,0:T(8,128)(2,1)}), bf16[32,24,128]{2,1,0:T(8,128)(2,1)S(1)}, u32[]{:S(2)}, u32[]{:S(2)}) %all-to-all-start) | async-done | bytes 196640 | tf_op jit(solution)/shard_map/all_to_all | solution.py:154
  20.1 4.3 %all-to-all-start.1 = ((bf16[16,160,128]{2,1,0:T(8,128)(2,1)}), bf16[16,160,128]{2,1,0:T(8,128)(2,1)S(1)}, u32[]{:S(2)}, u32[]{:S(2)}) async-start(bf16[16,160,128]{2,1,0:T(8,128)(2,1)} %shard_map.101), calls=%async_computation.1 | async-start | bytes 1310720 | tf_op jit(solution)/shard_map/all_to_all | solution.py:156
  24.5 2.2 %shard_map.102 = bf16[4,4,8,512]{3,2,1,0:T(8,128)(2,1)S(1)} custom-call(s32[1]{0:T(128)} %bitcast.own_ref, s32[1]{0:T(128)} %bitcast.1.zhi_ref, s32[32,32]{1,0:T(8,128)S(1)} %copy-done.1, s32[1024]{0:T(1024)S(1)} %copy-done.5, s32[32]{0:T(128)S(1)} %copy-done.6, bf16[32,24,128]{2,1,0:T(8,128)(2,1)S(1)} %all-to-all-done.got_ref, ...), custom_call_target="tpu_custom_call" | custom-call | flops 1073741824 | bytes 8388608 | tf_op jit(solution)/shard_map/pallas_call | solution.py:157
  26.7 13.7 %all-gather = bf16[16,4,8,512]{3,2,1,0:T(8,128)(2,1)S(1)} all-gather(bf16[4,4,8,512]{3,2,1,0:T(8,128)(2,1)S(1)} %shard_map.102), channel_id=2, replica_groups=mesh['z_lo'=4,'y'=4,'core'=2,'z_hi'=4,'x'=4] {'y'}, dimensions={0}, use_global_device_ids=true | all-gather | bytes 655360 | tf_op jit(solution)/shard_map/all_gather | solution.py:171
  40.4 1.0 all-to-all-done.1.near_ref
  41.4 3.8 %collective-permute-start = (bf16[16,160,128]{2,1,0:T(8,128)(2,1)S(1)}, bf16[16,160,128]{2,1,0:T(8,128)(2,1)S(1)}, u32[]{:S(2)}, u32[]{:S(2)}) collective-permute-start(bf16[16,160,128]{2,1,0:T(8,128)(2,1)S(1)} %all-to-all-done.1.near_ref), channel_id=1, source_target_pairs={{0,16},{16,0},{1,17},{17,1},{2,18},{18,2},{3,19},{19,3},{4,20},{20... | collective-permute-start | bytes 1966088 | tf_op jit(solution)/shard_map/ppermute | solution.py:173
  45.2 1.7 %collective-permute-done.far_ref = bf16[16,160,128]{2,1,0:T(8,128)(2,1)S(1)} collective-permute-done((bf16[16,160,128]{2,1,0:T(8,128)(2,1)S(1)}, bf16[16,160,128]{2,1,0:T(8,128)(2,1)S(1)}, u32[]{:S(2)}, u32[]{:S(2)}) %collective-permute-start) | collective-permute-done | bytes 655392 | tf_op jit(solution)/shard_map/ppermute | solution.py:173
  46.9 1.0 shard_map.103.w_ref
  47.9 0.8 shard_map.104
  48.7 24.4 %all_to_all.15 = bf16[16,32,1280]{2,1,0:T(8,128)(2,1)S(1)} all-to-all(bf16[16,32,1280]{2,1,0:T(8,128)(2,1)S(1)} %bitcast.28), channel_id=1, replica_groups=mesh['z_lo'=4,'y'=4,'core'=2,'z_hi'=4,'x'=4] {'x','y'}, dimensions={0} | all-to-all | bytes 2621440 | tf_op jit(solution)/shard_map/all_to_all | solution.py:192
  73.2 0.2 reduce_sum.12
  73.4 12.7 %collective-permute-start.1 = (bf16[4,8,1280]{2,1,0:T(8,128)(2,1)S(1)}, bf16[4,8,1280]{2,1,0:T(8,128)(2,1)S(1)}, u32[]{:S(2)}, u32[]{:S(2)}) collective-permute-start(bf16[4,8,1280]{2,1,0:T(8,128)(2,1)S(1)} %get-tuple-element.13), channel_id=1, source_target_pairs={{0,8},{4,12},{8,0},{12,4},{1,9},{5,13},{9,1},{13,5},{2,10},{6,14},... | collective-permute-start | bytes 245768 | tf_op jit(solution)/shard_map/ppermute | solution.py:195
  86.2 3.1 %collective-permute-start.3 = (bf16[4,8,1280]{2,1,0:T(8,128)(2,1)S(1)}, bf16[4,8,1280]{2,1,0:T(8,128)(2,1)S(1)}, u32[]{:S(2)}, u32[]{:S(2)}) collective-permute-start(bf16[4,8,1280]{2,1,0:T(8,128)(2,1)S(1)} %get-tuple-element.14), channel_id=1, source_target_pairs={{0,12},{4,0},{8,4},{12,8},{1,13},{5,1},{9,5},{13,9},{2,14},{6,2},{... | collective-permute-start | bytes 245768 | tf_op jit(solution)/shard_map/ppermute | solution.py:195
  89.3 6.1 %collective-permute-start.2 = (bf16[4,8,1280]{2,1,0:T(8,128)(2,1)S(1)}, bf16[4,8,1280]{2,1,0:T(8,128)(2,1)S(1)}, u32[]{:S(2)}, u32[]{:S(2)}) collective-permute-start(bf16[4,8,1280]{2,1,0:T(8,128)(2,1)S(1)} %get-tuple-element.15), channel_id=1, source_target_pairs={{0,4},{4,8},{8,12},{12,0},{1,5},{5,9},{9,13},{13,1},{2,6},{6,10},{... | collective-permute-start | bytes 245768 | tf_op jit(solution)/shard_map/ppermute | solution.py:195
  95.4 2.4 %collective-permute-done.3 = bf16[4,8,1280]{2,1,0:T(8,128)(2,1)S(1)} collective-permute-done((bf16[4,8,1280]{2,1,0:T(8,128)(2,1)S(1)}, bf16[4,8,1280]{2,1,0:T(8,128)(2,1)S(1)}, u32[]{:S(2)}, u32[]{:S(2)}) %collective-permute-start.3) | collective-permute-done | bytes 81952 | tf_op jit(solution)/shard_map/ppermute | solution.py:195
  97.8 6.6 %collective-permute-done.2 = bf16[4,8,1280]{2,1,0:T(8,128)(2,1)S(1)} collective-permute-done((bf16[4,8,1280]{2,1,0:T(8,128)(2,1)S(1)}, bf16[4,8,1280]{2,1,0:T(8,128)(2,1)S(1)}, u32[]{:S(2)}, u32[]{:S(2)}) %collective-permute-start.2) | collective-permute-done | bytes 81952 | tf_op jit(solution)/shard_map/ppermute | solution.py:195
  104.4 0.7 fusion.2
  (12 shorter events, 0.0 us)
Async XLA Ops:
  1.7 22.7 %copy-start.1 = (s32[32,32]{1,0:T(8,128)S(1)}, s32[32,32]{1,0:T(8,128)}, u32[]{:S(2)}) copy-start(s32[32,32]{1,0:T(8,128)} %serve_ref.1) | copy-start | bytes 12292
  1.7 22.7 %copy-start.5 = (s32[1024]{0:T(1024)S(1)}, s32[1024]{0:T(1024)}, u32[]{:S(2)}) copy-start(s32[1024]{0:T(1024)} %turn_ref.1) | copy-start | bytes 12292
  1.8 22.7 %copy-start.6 = (s32[32]{0:T(128)S(1)}, s32[32]{0:T(128)}, u32[]{:S(2)}) copy-start(s32[32]{0:T(128)} %cache_ref.1) | copy-start | bytes 388
  1.8 18.4 %all-to-all-start = ((bf16[32,24,128]{2,1,0:T(8,128)(2,1)}), bf16[32,24,128]{2,1,0:T(8,128)(2,1)S(1)}, u32[]{:S(2)}, u32[]{:S(2)}) async-start(bf16[32,24,128]{2,1,0:T(8,128)(2,1)} %shard_map.100), calls=%async_computation | async-start | bytes 393216 | tf_op jit(solution)/shard_map/all_to_all | solution.py:154
  11.3 0.9 copy-start
  12.2 12.3 %copy-start.3 = (bf16[32,128,128]{2,1,0:T(8,128)(2,1)S(1)}, bf16[32,128,128]{2,1,0:T(8,128)(2,1)}, u32[]{:S(2)}) copy-start(bf16[32,128,128]{2,1,0:T(8,128)(2,1)} %ck_ref.1) | copy-start | bytes 3145732
  12.2 12.3 %copy-start.4 = (bf16[32,128,128]{2,1,0:T(8,128)(2,1)S(1)}, bf16[32,128,128]{2,1,0:T(8,128)(2,1)}, u32[]{:S(2)}) copy-start(bf16[32,128,128]{2,1,0:T(8,128)(2,1)} %cv_ref.1) | copy-start | bytes 3145732
  20.1 21.3 %all-to-all-start.1 = ((bf16[16,160,128]{2,1,0:T(8,128)(2,1)}), bf16[16,160,128]{2,1,0:T(8,128)(2,1)S(1)}, u32[]{:S(2)}, u32[]{:S(2)}) async-start(bf16[16,160,128]{2,1,0:T(8,128)(2,1)} %shard_map.101), calls=%async_computation.1 | async-start | bytes 1310720 | tf_op jit(solution)/shard_map/all_to_all | solution.py:156
  24.5 22.4 %copy-start.2 = (s32[32]{0:T(128)S(1)}, s32[32]{0:T(128)}, u32[]{:S(2)}) copy-start(s32[32]{0:T(128)} %owner_ref.1) | copy-start | bytes 388
  41.4 5.5 %collective-permute-start = (bf16[16,160,128]{2,1,0:T(8,128)(2,1)S(1)}, bf16[16,160,128]{2,1,0:T(8,128)(2,1)S(1)}, u32[]{:S(2)}, u32[]{:S(2)}) collective-permute-start(bf16[16,160,128]{2,1,0:T(8,128)(2,1)S(1)} %all-to-all-done.1.near_ref), channel_id=1, source_target_pairs={{0,16},{16,0},{1,17},{17,1},{2,18},{18,2},{3,19},{19,3},{4,20},{20... | collective-permute-start | bytes 1966088 | tf_op jit(solution)/shard_map/ppermute | solution.py:173
  73.4 22.0 %collective-permute-start.1 = (bf16[4,8,1280]{2,1,0:T(8,128)(2,1)S(1)}, bf16[4,8,1280]{2,1,0:T(8,128)(2,1)S(1)}, u32[]{:S(2)}, u32[]{:S(2)}) collective-permute-start(bf16[4,8,1280]{2,1,0:T(8,128)(2,1)S(1)} %get-tuple-element.13), channel_id=1, source_target_pairs={{0,8},{4,12},{8,0},{12,4},{1,9},{5,13},{9,1},{13,5},{2,10},{6,14},... | collective-permute-start | bytes 245768 | tf_op jit(solution)/shard_map/ppermute | solution.py:195
  86.2 11.7 %collective-permute-start.3 = (bf16[4,8,1280]{2,1,0:T(8,128)(2,1)S(1)}, bf16[4,8,1280]{2,1,0:T(8,128)(2,1)S(1)}, u32[]{:S(2)}, u32[]{:S(2)}) collective-permute-start(bf16[4,8,1280]{2,1,0:T(8,128)(2,1)S(1)} %get-tuple-element.14), channel_id=1, source_target_pairs={{0,12},{4,0},{8,4},{12,8},{1,13},{5,1},{9,5},{13,9},{2,14},{6,2},{... | collective-permute-start | bytes 245768 | tf_op jit(solution)/shard_map/ppermute | solution.py:195
  89.3 15.1 %collective-permute-start.2 = (bf16[4,8,1280]{2,1,0:T(8,128)(2,1)S(1)}, bf16[4,8,1280]{2,1,0:T(8,128)(2,1)S(1)}, u32[]{:S(2)}, u32[]{:S(2)}) collective-permute-start(bf16[4,8,1280]{2,1,0:T(8,128)(2,1)S(1)} %get-tuple-element.15), channel_id=1, source_target_pairs={{0,4},{4,8},{8,12},{12,0},{1,5},{5,9},{9,13},{13,1},{2,6},{6,10},{... | collective-permute-start | bytes 245768 | tf_op jit(solution)/shard_map/ppermute | solution.py:195

commit v8 on v6

--- a/solution.py
+++ b/solution.py
@@ -51,7 +51,7 @@
             first = (y * blocks + j) * HD
             piece = w_ref[0, :, first : first + HD]
             for z in range(4):
-                out_ref[z * NCOL + y, j * OWN : (j + 1) * OWN, :] = piece
+                out_ref[y * 4 + z, j * OWN : (j + 1) * OWN, :] = piece
 
 
 def attend_kernel(own_ref, zhi_ref, serve_ref, turn_ref, cache_ref, got_ref, ck_ref, cv_ref, out_ref, nk, nv, s1, acc):
@@ -101,7 +101,7 @@
     for b in range(NREP):
         source = owner_ref[b]
         for j in range(out_ref.shape[1] // HD):
-            piece = both[source % 2, source // 2, j * OWN : (j + 1) * OWN, :]
+            piece = both[source % 2, source // 2 % NCOL * 4 + source // (2 * NCOL), j * OWN : (j + 1) * OWN, :]
             out_ref[b * OWN : (b + 1) * OWN, j * HD : (j + 1) * HD] = piece
 
 
@@ -153,7 +153,7 @@
     )(new_wo)
     got = lax.all_to_all(routed, REPL, split_axis=0, concat_axis=0, tiled=True)
     got, spread = lax.optimization_barrier((got, spread))
-    pieces = lax.all_to_all(spread, ("z_lo", "y"), split_axis=0, concat_axis=0, tiled=True)
+    pieces = lax.all_to_all(spread, ("y", "z_lo"), split_axis=0, concat_axis=0, tiled=True)
     attended = pl.pallas_call(
         attend_kernel,
         out_shape=jax.ShapeDtypeStruct((4, 4, 2 * TURN, HEADS * HD), jnp.bfloat16),

time: 106 us -> 104 us (0.981)
  the two profiles are of different devices: /device:TPU:33 before, /device:TPU:97 now
where the time goes in v8:
time: 104 us
  blocking collectives  40.3 us (39%)
  starting transfers between devices  40 us (38%)
  waiting for transfers between devices  14.4 us (14%)
  Pallas kernels  7.15 us (7%)
    all_to_all x1, blocking collectives, on_device(): lax.all_to_all(partial, ('x', 'y'), split_axis=0, concat_axis=0, tiled=True)  25.1 us
    ppermute x3, starting transfers between devices, on_device(): lax.ppermute(summed[d], 'z_hi', [(i, (i + d) % 4) for i in range(4)])  21.9 us
    all_gather x1, blocking collectives, on_device(): rows = lax.all_gather(attended, 'y', axis=0)  15.2 us
    all_to_all x1, starting transfers between devices, on_device(): got = lax.all_to_all(routed, REPL, split_axis=0, concat_axis=0, tiled=True)  8.7 us
    ppermute x3, waiting for transfers between devices, on_device(): lax.ppermute(summed[d], 'z_hi', [(i, (i + d) % 4) for i in range(4)])  6.89 us
    all_to_all x1, waiting for transfers between devices, on_device(): got = lax.all_to_all(routed, REPL, split_axis=0, concat_axis=0, tiled=True)  5.82 us
    all_to_all x1, starting transfers between devices, on_device(): lax.all_to_all(spread, ('y', 'z_lo'), split_axis=0, concat_axis=0, tiled=...  5.39 us
    ppermute x1, starting transfers between devices, on_device(): across = lax.ppermute(pieces, 'core', [(0, 1), (1, 0)])  3.92 us
  transfers between devices with their start and end apart: 6, of which 4 were waited for; matrix products, arithmetic and copies ran while one was open for 0% of the time, Pallas kernels for 3%

profile of v8, /device:TPU:97, one launch (start us, length us, event | category | flops | bytes accessed | tf_op | source)
XLA Modules:
  0.0 103.8 jit_solution(6514880980838804899)
XLA Ops:
  0.0 1.7 %shard_map.100 = bf16[32,24,128]{2,1,0:T(8,128)(2,1)} custom-call(s32[1]{0:T(128)} %bitcast.own_ref, s32[32,32]{1,0:T(8,128)} %serve_ref.1, bf16[32,4,512]{2,1,0:T(4,128)(2,1)} %q_hbm.1, bf16[32,4,128]{2,1,0:T(4,128)(2,1)} %k_hbm.1, bf16[32,4,128]{2,1,0:T(4,128)(2,1)} %v_hbm.1), custom_call_target="tpu_custom_call" | custom-call | tf_op jit(solution)/shard_map/pallas_call | solution.py:132
  1.7 0.0 copy-start.1
  1.7 0.0 copy-start.5
  1.8 0.0 copy-start.6
  1.8 8.7 %all-to-all-start = ((bf16[32,24,128]{2,1,0:T(8,128)(2,1)}), bf16[32,24,128]{2,1,0:T(8,128)(2,1)S(1)}, u32[]{:S(2)}, u32[]{:S(2)}) async-start(bf16[32,24,128]{2,1,0:T(8,128)(2,1)} %shard_map.100), calls=%async_computation | async-start | bytes 393216 | tf_op jit(solution)/shard_map/all_to_all | solution.py:154
  10.5 0.0 copy-start
  10.5 0.9 copy-done
  11.4 0.9 shard_map.101
  12.3 5.8 %all-to-all-done.got_ref = bf16[32,24,128]{2,1,0:T(8,128)(2,1)S(1)} async-done(((bf16[32,24,128]{2,1,0:T(8,128)(2,1)}), bf16[32,24,128]{2,1,0:T(8,128)(2,1)S(1)}, u32[]{:S(2)}, u32[]{:S(2)}) %all-to-all-start) | async-done | bytes 196640 | tf_op jit(solution)/shard_map/all_to_all | solution.py:154
  18.2 5.4 %all-to-all-start.1 = ((bf16[16,160,128]{2,1,0:T(8,128)(2,1)}), bf16[16,160,128]{2,1,0:T(8,128)(2,1)S(1)}, u32[]{:S(2)}, u32[]{:S(2)}) async-start(bf16[16,160,128]{2,1,0:T(8,128)(2,1)} %shard_map.101), calls=%async_computation.1 | async-start | bytes 1310720 | tf_op jit(solution)/shard_map/all_to_all | solution.py:156
  23.6 2.2 %shard_map.102 = bf16[4,4,8,512]{3,2,1,0:T(8,128)(2,1)S(1)} custom-call(s32[1]{0:T(128)} %bitcast.own_ref, s32[1]{0:T(128)} %bitcast.1.zhi_ref, s32[32,32]{1,0:T(8,128)S(1)} %copy-done.1, s32[1024]{0:T(1024)S(1)} %copy-done.5, s32[32]{0:T(128)S(1)} %copy-done.6, bf16[32,24,128]{2,1,0:T(8,128)(2,1)S(1)} %all-to-all-done.got_ref, ...), custom_call_target="tpu_custom_call" | custom-call | flops 1073741824 | bytes 8388608 | tf_op jit(solution)/shard_map/pallas_call | solution.py:157
  25.8 15.2 %all-gather = bf16[16,4,8,512]{3,2,1,0:T(8,128)(2,1)S(1)} all-gather(bf16[4,4,8,512]{3,2,1,0:T(8,128)(2,1)S(1)} %shard_map.102), channel_id=2, replica_groups=mesh['z_lo'=4,'y'=4,'core'=2,'z_hi'=4,'x'=4] {'y'}, dimensions={0}, use_global_device_ids=true | all-gather | bytes 655360 | tf_op jit(solution)/shard_map/all_gather | solution.py:171
  41.1 3.9 %collective-permute-start = (bf16[16,160,128]{2,1,0:T(8,128)(2,1)S(1)}, bf16[16,160,128]{2,1,0:T(8,128)(2,1)S(1)}, u32[]{:S(2)}, u32[]{:S(2)}) collective-permute-start(bf16[16,160,128]{2,1,0:T(8,128)(2,1)S(1)} %all-to-all-done.1.near_ref), channel_id=1, source_target_pairs={{0,16},{16,0},{1,17},{17,1},{2,18},{18,2},{3,19},{19,3},{4,20},{20... | collective-permute-start | bytes 1966088 | tf_op jit(solution)/shard_map/ppermute | solution.py:173
  45.0 1.7 %collective-permute-done.far_ref = bf16[16,160,128]{2,1,0:T(8,128)(2,1)S(1)} collective-permute-done((bf16[16,160,128]{2,1,0:T(8,128)(2,1)S(1)}, bf16[16,160,128]{2,1,0:T(8,128)(2,1)S(1)}, u32[]{:S(2)}, u32[]{:S(2)}) %collective-permute-start) | collective-permute-done | bytes 655392 | tf_op jit(solution)/shard_map/ppermute | solution.py:173
  46.7 1.2 %shard_map.103.w_ref = bf16[512,1280]{1,0:T(8,128)(2,1)S(1)} custom-call(s32[32]{0:T(128)S(1)} %copy-done.2, s32[1]{0:T(128)} %bitcast.4.core_ref, bf16[16,160,128]{2,1,0:T(8,128)(2,1)S(1)} %all-to-all-done.1.near_ref, bf16[16,160,128]{2,1,0:T(8,128)(2,1)S(1)} %collective-permute-done.far_ref), custom_call_target="tpu_custom_call" | custom-call | bytes 2621440 | tf_op jit(solution)/shard_map/pallas_call | solution.py:174
  47.9 1.1 %shard_map.104 = bf16[4,4,32,1280]{3,2,1,0:T(8,128)(2,1)S(1)} custom-call(bf16[512,512]{1,0:T(8,128)(2,1)S(1)} %bitcast.29, bf16[512,1280]{1,0:T(8,128)(2,1)S(1)} %shard_map.103.w_ref), custom_call_target="tpu_custom_call" | custom-call | tf_op jit(solution)/shard_map/pallas_call | solution.py:184
  49.0 25.1 %all_to_all.15 = bf16[16,32,1280]{2,1,0:T(8,128)(2,1)S(1)} all-to-all(bf16[16,32,1280]{2,1,0:T(8,128)(2,1)S(1)} %bitcast.28), channel_id=1, replica_groups=mesh['z_lo'=4,'y'=4,'core'=2,'z_hi'=4,'x'=4] {'x','y'}, dimensions={0} | all-to-all | bytes 2621440 | tf_op jit(solution)/shard_map/all_to_all | solution.py:196
  74.1 0.2 reduce_sum.12
  74.3 12.7 %collective-permute-start.1 = (bf16[4,8,1280]{2,1,0:T(8,128)(2,1)S(1)}, bf16[4,8,1280]{2,1,0:T(8,128)(2,1)S(1)}, u32[]{:S(2)}, u32[]{:S(2)}) collective-permute-start(bf16[4,8,1280]{2,1,0:T(8,128)(2,1)S(1)} %get-tuple-element.13), channel_id=1, source_target_pairs={{0,8},{4,12},{8,0},{12,4},{1,9},{5,13},{9,1},{13,5},{2,10},{6,14},... | collective-permute-start | bytes 245768 | tf_op jit(solution)/shard_map/ppermute | solution.py:199
  87.0 3.1 %collective-permute-start.3 = (bf16[4,8,1280]{2,1,0:T(8,128)(2,1)S(1)}, bf16[4,8,1280]{2,1,0:T(8,128)(2,1)S(1)}, u32[]{:S(2)}, u32[]{:S(2)}) collective-permute-start(bf16[4,8,1280]{2,1,0:T(8,128)(2,1)S(1)} %get-tuple-element.14), channel_id=1, source_target_pairs={{0,12},{4,0},{8,4},{12,8},{1,13},{5,1},{9,5},{13,9},{2,14},{6,2},{... | collective-permute-start | bytes 245768 | tf_op jit(solution)/shard_map/ppermute | solution.py:199
  90.1 6.1 %collective-permute-start.2 = (bf16[4,8,1280]{2,1,0:T(8,128)(2,1)S(1)}, bf16[4,8,1280]{2,1,0:T(8,128)(2,1)S(1)}, u32[]{:S(2)}, u32[]{:S(2)}) collective-permute-start(bf16[4,8,1280]{2,1,0:T(8,128)(2,1)S(1)} %get-tuple-element.15), channel_id=1, source_target_pairs={{0,4},{4,8},{8,12},{12,0},{1,5},{5,9},{9,13},{13,1},{2,6},{6,10},{... | collective-permute-start | bytes 245768 | tf_op jit(solution)/shard_map/ppermute | solution.py:199
  96.3 3.9 %collective-permute-done.3 = bf16[4,8,1280]{2,1,0:T(8,128)(2,1)S(1)} collective-permute-done((bf16[4,8,1280]{2,1,0:T(8,128)(2,1)S(1)}, bf16[4,8,1280]{2,1,0:T(8,128)(2,1)S(1)}, u32[]{:S(2)}, u32[]{:S(2)}) %collective-permute-start.3) | collective-permute-done | bytes 81952 | tf_op jit(solution)/shard_map/ppermute | solution.py:199
  100.1 3.0 %collective-permute-done.2 = bf16[4,8,1280]{2,1,0:T(8,128)(2,1)S(1)} collective-permute-done((bf16[4,8,1280]{2,1,0:T(8,128)(2,1)S(1)}, bf16[4,8,1280]{2,1,0:T(8,128)(2,1)S(1)}, u32[]{:S(2)}, u32[]{:S(2)}) %collective-permute-start.2) | collective-permute-done | bytes 81952 | tf_op jit(solution)/shard_map/ppermute | solution.py:199
  103.1 0.7 fusion.2
  (12 shorter events, 0.0 us)
Async XLA Ops:
  1.7 21.8 %copy-start.1 = (s32[32,32]{1,0:T(8,128)S(1)}, s32[32,32]{1,0:T(8,128)}, u32[]{:S(2)}) copy-start(s32[32,32]{1,0:T(8,128)} %serve_ref.1) | copy-start | bytes 12292
  1.7 21.8 %copy-start.5 = (s32[1024]{0:T(1024)S(1)}, s32[1024]{0:T(1024)}, u32[]{:S(2)}) copy-start(s32[1024]{0:T(1024)} %turn_ref.1) | copy-start | bytes 12292
  1.8 21.8 %copy-start.6 = (s32[32]{0:T(128)S(1)}, s32[32]{0:T(128)}, u32[]{:S(2)}) copy-start(s32[32]{0:T(128)} %cache_ref.1) | copy-start | bytes 388
  1.8 16.4 %all-to-all-start = ((bf16[32,24,128]{2,1,0:T(8,128)(2,1)}), bf16[32,24,128]{2,1,0:T(8,128)(2,1)S(1)}, u32[]{:S(2)}, u32[]{:S(2)}) async-start(bf16[32,24,128]{2,1,0:T(8,128)(2,1)} %shard_map.100), calls=%async_computation | async-start | bytes 393216 | tf_op jit(solution)/shard_map/all_to_all | solution.py:154
  10.5 0.9 copy-start
  11.4 12.2 %copy-start.3 = (bf16[32,128,128]{2,1,0:T(8,128)(2,1)S(1)}, bf16[32,128,128]{2,1,0:T(8,128)(2,1)}, u32[]{:S(2)}) copy-start(bf16[32,128,128]{2,1,0:T(8,128)(2,1)} %ck_ref.1) | copy-start | bytes 3145732
  11.4 12.2 %copy-start.4 = (bf16[32,128,128]{2,1,0:T(8,128)(2,1)S(1)}, bf16[32,128,128]{2,1,0:T(8,128)(2,1)}, u32[]{:S(2)}) copy-start(bf16[32,128,128]{2,1,0:T(8,128)(2,1)} %cv_ref.1) | copy-start | bytes 3145732
  18.2 22.9 %all-to-all-start.1 = ((bf16[16,160,128]{2,1,0:T(8,128)(2,1)}), bf16[16,160,128]{2,1,0:T(8,128)(2,1)S(1)}, u32[]{:S(2)}, u32[]{:S(2)}) async-start(bf16[16,160,128]{2,1,0:T(8,128)(2,1)} %shard_map.101), calls=%async_computation.1 | async-start | bytes 1310720 | tf_op jit(solution)/shard_map/all_to_all | solution.py:156
  23.6 23.1 %copy-start.2 = (s32[32]{0:T(128)S(1)}, s32[32]{0:T(128)}, u32[]{:S(2)}) copy-start(s32[32]{0:T(128)} %owner_ref.1) | copy-start | bytes 388
  41.1 5.6 %collective-permute-start = (bf16[16,160,128]{2,1,0:T(8,128)(2,1)S(1)}, bf16[16,160,128]{2,1,0:T(8,128)(2,1)S(1)}, u32[]{:S(2)}, u32[]{:S(2)}) collective-permute-start(bf16[16,160,128]{2,1,0:T(8,128)(2,1)S(1)} %all-to-all-done.1.near_ref), channel_id=1, source_target_pairs={{0,16},{16,0},{1,17},{17,1},{2,18},{18,2},{3,19},{19,3},{4,20},{20... | collective-permute-start | bytes 1966088 | tf_op jit(solution)/shard_map/ppermute | solution.py:173
  74.3 22.0 %collective-permute-start.1 = (bf16[4,8,1280]{2,1,0:T(8,128)(2,1)S(1)}, bf16[4,8,1280]{2,1,0:T(8,128)(2,1)S(1)}, u32[]{:S(2)}, u32[]{:S(2)}) collective-permute-start(bf16[4,8,1280]{2,1,0:T(8,128)(2,1)S(1)} %get-tuple-element.13), channel_id=1, source_target_pairs={{0,8},{4,12},{8,0},{12,4},{1,9},{5,13},{9,1},{13,5},{2,10},{6,14},... | collective-permute-start | bytes 245768 | tf_op jit(solution)/shard_map/ppermute | solution.py:199
  87.0 13.1 %collective-permute-start.3 = (bf16[4,8,1280]{2,1,0:T(8,128)(2,1)S(1)}, bf16[4,8,1280]{2,1,0:T(8,128)(2,1)S(1)}, u32[]{:S(2)}, u32[]{:S(2)}) collective-permute-start(bf16[4,8,1280]{2,1,0:T(8,128)(2,1)S(1)} %get-tuple-element.14), channel_id=1, source_target_pairs={{0,12},{4,0},{8,4},{12,8},{1,13},{5,1},{9,5},{13,9},{2,14},{6,2},{... | collective-permute-start | bytes 245768 | tf_op jit(solution)/shard_map/ppermute | solution.py:199
  90.1 13.0 %collective-permute-start.2 = (bf16[4,8,1280]{2,1,0:T(8,128)(2,1)S(1)}, bf16[4,8,1280]{2,1,0:T(8,128)(2,1)S(1)}, u32[]{:S(2)}, u32[]{:S(2)}) collective-permute-start(bf16[4,8,1280]{2,1,0:T(8,128)(2,1)S(1)} %get-tuple-element.15), channel_id=1, source_target_pairs={{0,4},{4,8},{8,12},{12,0},{1,5},{5,9},{9,13},{13,1},{2,6},{6,10},{... | collective-permute-start | bytes 245768 | tf_op jit(solution)/shard_map/ppermute | solution.py:199
